TPU v7x, 32 devices: a whole 2x2x4 slice. The times are simulated.
32 devices in a mesh: particle: 4 (over x, core), rows: 8 (over z, y).
Axes of the slice: x: 2, y: 2, z: 4, core: 2. Of those that a mesh axis runs over, the one named last changes fastest.
Arguments:
- latent: bfloat16 [4, 32, 24, 640], P('particle', 'rows'), may hold values from -20 to 20
- ada_scale: float32 [640], replicated, may hold values from -0.5 to 0.5
- ada_shift: float32 [640], replicated, may hold values from -3 to 3
- conv_weight: bfloat16 [5760, 640], P('rows'), may hold values from -0.078125 to 0.078125
- qkv_weight: bfloat16 [640, 1920], replicated, may hold values from -1.4230249 to 1.4230249
- out_weight: bfloat16 [640, 640], replicated, may hold values from -0.25 to 0.25
- ancestors: int32 [4], replicated, may hold values from 0 to 3
Outputs:
- resampled: bfloat16 [4, 32, 24, 640], P('particle', 'rows')
All inputs are finite; a program needn't handle non-finite values.
Results may differ from a plain program's by a relative error of at most 0.0081.
Values may be sent and summed in bfloat16 or wider, within the bound.
A program may use at most 64 MiB of HBM per device.

v0:
```python
import functools
import math

import jax
import jax.numpy as jnp
from jax import lax
from jax.experimental import pallas as pl
from jax.experimental.pallas import tpu as pltpu
from jax.sharding import PartitionSpec as P

HEADS = 10
GROUPS = 32
INNER = 2
LANES = 128
MESH = pl.DeviceIdType.MESH


def kernel(
    dims,
    anc_ref,
    x_ref,
    scale_ref,
    shift_ref,
    wconv_hbm,
    wqkv_hbm,
    wout_hbm,
    out_ref,
    wconv,
    wqkv,
    wout,
    lat,
    shifted,
    ysend,
    yrecv,
    zsend,
    zrecv,
    own,
    res,
    normed,
    kv,
    att,
    blk,
    blocks,
    stat,
    load_sem,
    up1,
    down1,
    ys1,
    rv1,
    rys,
    ryr,
    rzs,
    rzr,
    up2,
    down2,
    ys2,
    rv2,
    ps,
    pr,
):
    rows_here, width, chans, ranks, particles, taps, share = dims
    tokens = rows_here * width
    outer = ranks // INNER
    count = tokens * ranks * (chans // GROUPS)
    head_dim = chans // HEADS
    me = lax.axis_index("rows")
    mine = lax.axis_index("particle")
    a = lax.div(me, INNER)
    b = lax.rem(me, INNER)
    other = a * INNER + (1 - b)

    def ahead(k):
        return lax.rem(a + k, outer)

    def behind(k):
        return lax.rem(a + outer - k, outer)

    padded = wconv_hbm.shape[0] == wconv.shape[0]
    if padded:
        weights_in = wconv
    else:
        grain = math.gcd(share, chans)
        skip = lax.rem(me * (share // grain), chans // grain)
        weights_in = wconv.at[pl.ds(pl.multiple_of(skip * grain, grain), share)]
    loads = [
        pltpu.make_async_copy(wconv_hbm, weights_in, load_sem.at[0]),
        pltpu.make_async_copy(wqkv_hbm, wqkv, load_sem.at[1]),
        pltpu.make_async_copy(wout_hbm, wout, load_sem.at[2]),
    ]
    for load in loads:
        load.start()

    if not padded:
        for i in range(taps * chans // grain):

            @pl.when((skip > i) | (skip + share // grain <= i))
            def _():
                wconv[i * grain : (i + 1) * grain] = jnp.zeros((grain, chans), wconv.dtype)

    barrier = pltpu.get_barrier_semaphore()
    pl.semaphore_signal(barrier, inc=1, device_id={"rows": other}, device_id_type=MESH)
    for k in range(1, outer):
        pl.semaphore_signal(
            barrier, inc=1, device_id={"rows": ahead(k) * INNER + b}, device_id_type=MESH
        )
    for k in range(1, particles):
        pl.semaphore_signal(
            barrier,
            inc=1,
            device_id={"particle": lax.rem(mine + k, particles)},
            device_id_type=MESH,
        )
    pl.semaphore_wait(barrier, outer + particles - 1)

    def to_row(src, dst, send, recv, row):
        return pltpu.make_async_remote_copy(
            src_ref=src,
            dst_ref=dst,
            send_sem=send,
            recv_sem=recv,
            device_id={"rows": row},
            device_id_type=MESH,
        )

    half = tokens // 2

    def part_of(buf, slot, piece):
        return buf.at[slot, pl.ds(piece * half, half)]

    def gather(src, buf, up, down, across, rv):
        stat[...] = jnp.zeros_like(stat)

        def add(slot):
            v = buf[slot].astype(jnp.float32)
            stat[0:1] += jnp.sum(v, axis=0, keepdims=True)
            stat[1:2] += jnp.sum(v * v, axis=0, keepdims=True)

        def copy(slot, piece, sems, row, mine_too=False):
            here = src.at[pl.ds(piece * half, half)] if mine_too else part_of(buf, slot, piece)
            return to_row(
                here, part_of(buf, slot, piece), sems.at[slot, piece], rv.at[slot, piece], row
            )

        def both(slot, piece, act, own_too=False):
            @pl.when(a + 1 < outer)
            def _():
                act(copy(slot, piece, up, (a + 1) * INNER + b, own_too))

            @pl.when(a > 0)
            def _():
                act(copy(slot, piece, down, (a - 1) * INNER + b, own_too))

        def start(c):
            c.start()

        def done(c):
            c.wait_send()

        def arrived(slot, piece):
            copy(slot, piece, across, other).wait_recv()

        copy(me, 1, across, other, True).start()
        both(me, 0, start, True)
        both(me, 1, start, True)
        copy(me, 0, across, other, True).start()
        buf[me] = src[...]
        add(me)
        arrived(other, 1)
        both(other, 1, start)
        for t in range(1, outer):
            sides = (
                (a >= t, a - t, a + 1 < outer, up, a + 1),
                (a + t < outer, a + t, a > 0, down, a - 1),
            )
            for present, origin, onward, sems, target in sides:
                near = origin * INNER + b
                far = origin * INNER + (1 - b)
                row = target * INNER + b
                for slot, piece in ((near, 0), (near, 1), (far, 1)):

                    @pl.when(present)
                    def _():
                        arrived(slot, piece)

                    @pl.when(present & onward)
                    def _():
                        copy(slot, piece, sems, row).start()

                    if piece == 0:

                        @pl.when(present)
                        def _():
                            copy(slot, piece, across, other).start()

                @pl.when(present)
                def _():
                    add(near)

        arrived(other, 0)
        add(other)
        for t in range(1, outer):
            for present, origin in ((a >= t, a - t), (a + t < outer, a + t)):

                @pl.when(present)
                def _():
                    slot = origin * INNER + (1 - b)
                    arrived(slot, 0)
                    add(slot)

        def finish_sends():
            copy(me, 1, across, other, True).wait_send()
            copy(me, 0, across, other, True).wait_send()
            both(me, 0, done, True)
            both(me, 1, done, True)
            both(other, 1, done)
            for t in range(1, outer):
                sides = (
                    (a >= t, a - t, a + 1 < outer, up, a + 1),
                    (a + t < outer, a + t, a > 0, down, a - 1),
                )
                for present, origin, onward, sems, target in sides:
                    near = origin * INNER + b
                    far = origin * INNER + (1 - b)
                    row = target * INNER + b

                    @pl.when(present & onward)
                    def _():
                        for slot, piece in ((near, 0), (near, 1), (far, 1)):
                            copy(slot, piece, sems, row).wait_send()

                    @pl.when(present)
                    def _():
                        copy(near, 0, across, other).wait_send()

        return stat[0:1], stat[1:2], finish_sends

    per_group = chans // GROUPS
    chan_r = lax.broadcasted_iota(jnp.int32, (chans, LANES), 0)
    group_r = lax.broadcasted_iota(jnp.int32, (chans, LANES), 1) * per_group
    inside = (chan_r >= group_r) & (chan_r < group_r + per_group)
    to_group = jnp.where(inside, 1.0, 0.0).astype(jnp.float32)
    group_c = lax.broadcasted_iota(jnp.int32, (LANES, chans), 0) * per_group
    chan_c = lax.broadcasted_iota(jnp.int32, (LANES, chans), 1)
    inside = (chan_c >= group_c) & (chan_c < group_c + per_group)
    to_chan = jnp.where(inside, 1.0, 0.0).astype(jnp.float32)

    def finish(total, square):
        stacked = jnp.concatenate(
            [total, square, jnp.zeros((6, chans), jnp.float32)], axis=0
        )
        by_group = (
            jnp.dot(
                stacked,
                to_group,
                precision=lax.Precision.HIGHEST,
                preferred_element_type=jnp.float32,
            )
            / count
        )
        mean_g = by_group[0:1]
        inverse = lax.rsqrt(by_group[1:2] - mean_g * mean_g + 1e-05)
        back = jnp.concatenate(
            [mean_g, inverse, jnp.zeros((6, LANES), jnp.float32)], axis=0
        )
        spread = jnp.dot(
            back,
            to_chan,
            precision=lax.Precision.HIGHEST,
            preferred_element_type=jnp.float32,
        )
        return spread[0:1], spread[1:2]

    total, square, finish_first = gather(x_ref, lat, up1, down1, ys1, rv1)
    sends = []
    mean_c, inverse_c = finish(total, square)
    gain = 1.0 + scale_ref[...].reshape(1, chans)
    bias = shift_ref[...].reshape(1, chans)
    first = lax.div(me * share, chans)
    tap_ids = [jnp.minimum(first + j, 8) for j in range(taps)]
    column = lax.broadcasted_iota(
        jnp.int32, (rows_here, width, chans), 1
    ).reshape(tokens, chans)
    edge = jnp.zeros((1, width, chans), jnp.float32)
    for j in range(taps):
        shifted[j, 0:1] = edge
        shifted[j, ranks * rows_here + 1 : ranks * rows_here + 2] = edge

    def activate(s, carry):
        v = lat[s].astype(jnp.float32)
        v = (v - mean_c) * inverse_c * gain + bias
        v = (v / (1.0 + jnp.exp(-v))).astype(jnp.bfloat16).astype(jnp.float32)
        left = jnp.where(column == 0, 0.0, pltpu.roll(v, 1, 0))
        right = jnp.where(column == width - 1, 0.0, pltpu.roll(v, tokens - 1, 0))
        for j in range(taps):
            off = lax.rem(tap_ids[j], 3)
            w = jnp.where(off == 0, left, jnp.where(off == 2, right, v))
            shifted[j, pl.ds(1 + s * rows_here, rows_here)] = w.reshape(
                rows_here, width, chans
            )
        return carry

    lax.fori_loop(0, ranks, activate, 0)
    loads[0].wait()

    def conv(slot):
        acc = None
        for j in range(taps):
            window = shifted[j, pl.ds(slot * rows_here + lax.div(tap_ids[j], 3), rows_here)]
            part = jnp.dot(
                window.reshape(tokens, chans).astype(jnp.bfloat16),
                wconv[j * chans : (j + 1) * chans],
                preferred_element_type=jnp.float32,
            )
            acc = part if acc is None else acc + part
        return acc

    order = list(range(1, outer)) + [0]
    for i, k in enumerate(order):
        ysend[i] = conv(ahead(k) * INNER + (1 - b)).astype(jnp.bfloat16)
        sends.append(to_row(ysend.at[i], yrecv.at[i], rys.at[i], ryr.at[i], other))
        sends[-1].start()
    for i, k in enumerate(order):
        part = conv(ahead(k) * INNER + b)
        to_row(ysend.at[i], yrecv.at[i], rys.at[i], ryr.at[i], other).wait_recv()
        part = part + yrecv[i].astype(jnp.float32)
        if k > 0:
            zsend[i] = part.astype(jnp.bfloat16)
            sends.append(
                to_row(
                    zsend.at[i], zrecv.at[i], rzs.at[i], rzr.at[i], ahead(k) * INNER + b
                )
            )
            sends[-1].start()
    for i in range(outer - 1):
        to_row(zsend.at[i], zrecv.at[i], rzs.at[i], rzr.at[i], me).wait_recv()
        part = part + zrecv[i].astype(jnp.float32)
    own[...] = (x_ref[...].astype(jnp.float32) + part).astype(jnp.bfloat16)

    total, square, finish_second = gather(own, res, up2, down2, ys2, rv2)
    mean_m, inverse_m = finish(total, square)

    def normalize(s, carry):
        v = (res[s].astype(jnp.float32) - mean_m) * inverse_m
        normed[pl.ds(pl.multiple_of(s * tokens, tokens), tokens)] = v.astype(jnp.bfloat16)
        return carry

    lax.fori_loop(0, ranks, normalize, 0)
    loads[1].wait()
    mine_n = ((own[...].astype(jnp.float32) - mean_m) * inverse_m).astype(jnp.bfloat16)
    query = jnp.dot(
        mine_n, wqkv[:, :chans], preferred_element_type=jnp.float32
    ).astype(jnp.bfloat16)
    step = 2 * LANES
    for n in range(2 * chans // step):
        kv[:, n * step : (n + 1) * step] = jnp.dot(
            normed[...],
            wqkv[:, chans + n * step : chans + (n + 1) * step],
            preferred_element_type=jnp.float32,
        ).astype(jnp.bfloat16)

    pair = 2 * head_dim
    lane = lax.broadcasted_iota(jnp.int32, (tokens, pair), 1)
    low = lane < head_dim
    zero = jnp.zeros((tokens, pair), jnp.bfloat16)
    for h in range(HEADS // 2):
        q = query[:, h * pair : (h + 1) * pair]
        q = jnp.concatenate([jnp.where(low, q, zero), jnp.where(low, zero, q)], axis=0)
        scores = lax.dot_general(
            q,
            kv[:, h * pair : (h + 1) * pair],
            (((1,), (1,)), ((), ())),
            preferred_element_type=jnp.float32,
        ) * (head_dim ** (-0.5))
        top = jnp.max(scores, axis=1, keepdims=True)
        weights = jnp.exp(scores - top)
        norm = jnp.sum(weights, axis=1, keepdims=True)
        mixed = (
            jnp.dot(
                weights.astype(jnp.bfloat16),
                kv[:, chans + h * pair : chans + (h + 1) * pair],
                preferred_element_type=jnp.float32,
            )
            / norm
        )
        att[:, h * pair : (h + 1) * pair] = jnp.where(
            low, mixed[:tokens], mixed[tokens:]
        ).astype(jnp.bfloat16)
    loads[2].wait()
    block = (
        own[...].astype(jnp.float32)
        + jnp.dot(att[...], wout[...], preferred_element_type=jnp.float32)
    ).astype(jnp.bfloat16)
    blk[...] = block
    blocks[mine] = block

    def to_particle(k):
        peer = lax.rem(mine + k, particles)
        return pltpu.make_async_remote_copy(
            src_ref=blk,
            dst_ref=blocks.at[mine],
            send_sem=ps.at[k - 1],
            recv_sem=pr.at[k - 1],
            device_id={"particle": peer},
            device_id_type=MESH,
        )

    for k in range(1, particles):
        sends.append(to_particle(k))
        sends[-1].start()
    for k in range(1, particles):
        to_particle(k).wait_recv()
    out_ref[...] = blocks[anc_ref[mine]]
    for send in sends:
        send.wait_send()
    finish_first()
    finish_second()


def per_device(latent, ada_scale, ada_shift, conv_weight, qkv_weight, out_weight, ancestors):
    _, rows_here, width, chans = latent.shape
    tokens = rows_here * width
    ranks = lax.axis_size("rows")
    particles = lax.axis_size("particle")
    outer = ranks // INNER
    share = conv_weight.shape[0]
    taps = max(-(-((r * share) % chans + share) // chans) for r in range(ranks))
    wpad = conv_weight
    if math.gcd(share, chans) % 16:
        start = lax.rem(lax.axis_index("rows") * share, chans)
        wpad = lax.dynamic_update_slice(
            jnp.zeros((taps * chans, chans), wpad.dtype), wpad, (start, 0)
        )
    dims = (rows_here, width, chans, ranks, particles, taps, share)
    bf16, f32 = jnp.bfloat16, jnp.float32
    dma = pltpu.SemaphoreType.DMA
    out = pl.pallas_call(
        functools.partial(kernel, dims),
        out_shape=jax.ShapeDtypeStruct((tokens, chans), bf16),
        in_specs=[pl.BlockSpec(memory_space=pltpu.SMEM)]
        + [pl.BlockSpec(memory_space=pltpu.VMEM)] * 3
        + [pl.BlockSpec(memory_space=pl.ANY)] * 3,
        out_specs=pl.BlockSpec(memory_space=pltpu.VMEM),
        scratch_shapes=[
            pltpu.VMEM((taps * chans, chans), bf16),
            pltpu.VMEM(qkv_weight.shape, bf16),
            pltpu.VMEM(out_weight.shape, bf16),
            pltpu.VMEM((ranks, tokens, chans), bf16),
            pltpu.VMEM((taps, ranks * rows_here + 2, width, chans), f32),
            pltpu.VMEM((outer, tokens, chans), bf16),
            pltpu.VMEM((outer, tokens, chans), bf16),
            pltpu.VMEM((outer, tokens, chans), bf16),
            pltpu.VMEM((outer, tokens, chans), bf16),
            pltpu.VMEM((tokens, chans), bf16),
            pltpu.VMEM((ranks, tokens, chans), bf16),
            pltpu.VMEM((ranks * tokens, chans), bf16),
            pltpu.VMEM((ranks * tokens, 2 * chans), bf16),
            pltpu.VMEM((tokens, chans), bf16),
            pltpu.VMEM((tokens, chans), bf16),
            pltpu.VMEM((particles, tokens, chans), bf16),
            pltpu.VMEM((8, chans), f32),
            dma((3,)),
            dma((ranks, 2)),
            dma((ranks, 2)),
            dma((ranks, 2)),
            dma((ranks, 2)),
            dma((outer,)),
            dma((outer,)),
            dma((outer,)),
            dma((outer,)),
            dma((ranks, 2)),
            dma((ranks, 2)),
            dma((ranks, 2)),
            dma((ranks, 2)),
            dma((particles,)),
            dma((particles,)),
        ],
        compiler_params=pltpu.CompilerParams(
            collective_id=0, has_side_effects=True, vmem_limit_bytes=60000 * 1024
        ),
        name="block",
    )(
        ancestors,
        latent.reshape(tokens, chans),
        ada_scale,
        ada_shift,
        wpad,
        qkv_weight,
        out_weight,
    )
    return out.reshape(latent.shape)


def solution(mesh):
    in_specs = (P("particle", "rows", None, None), P(), P(), P("rows", None), P(), P(), P())
    out_specs = P("particle", "rows", None, None)
    return jax.shard_map(
        per_device, mesh=mesh, in_specs=in_specs, out_specs=out_specs, check_vma=False
    )
```

profile of v0, /device:TPU:0, one launch (start us, length us, event | category | flops | bytes accessed | tf_op | source)
XLA Modules:
  0.0 65.4 jit_solution(2316680044543927309)
XLA Ops:
  0.0 63.9 %block.1 = bf16[96,640]{1,0:T(8,128)(2,1)} custom-call(s32[4]{0:T(128)} %anc_ref.1, bf16[96,640]{1,0:T(8,128)(2,1)} %bitcast.3, f32[640]{0:T(1024)} %scale_ref.1, f32[640]{0:T(1024)} %shift_ref.1, bf16[720,640]{1,0:T(8,128)(2,1)} %wconv_hbm.1, bf16[640,1920]{1,0:T(8,128)(2,1)} %wqkv_hbm.1, bf16[640,640]{1,0:T(8,128)(2,1)} %wout_hbm.1), custom_call_target="tpu_custom_call" | custom-call | tf_op jit(solution)/shard_map/block/pallas_call | solution.py:436
  63.9 1.6 %copy.9 = bf16[1,4,24,640]{3,2,1,0:T(8,128)(2,1)} copy(bf16[1,4,24,640]{3,2,1,0:T(8,128)(2,1)} %bitcast.2) | data formatting | bytes 245760
where the time goes:
time: 66.2 us; the launch traced here: 65.4 us
  Pallas kernels  63.9 us (97%)
  local copies, waits for them, and re-layouts  1.56 us (2%)
    pallas_call x1, Pallas kernels, per_device(): pl.pallas_call(functools.partial(kernel, dims), out_shape=jax.ShapeDtypeS...  63.9 us
    unnamed x1, local copies, waits for them, and re-layouts  1.56 us

commit v1 on v0

v1 whole, which is shorter than its diff:
```python
import functools
import math

import jax
import jax.numpy as jnp
from jax import lax
from jax.experimental import pallas as pl
from jax.experimental.pallas import tpu as pltpu
from jax.sharding import PartitionSpec as P

HEADS = 10
GROUPS = 32
INNER = 2
CORES = 2
LANES = 128
GRAIN = 16
TAPS = 9
MESH = pl.DeviceIdType.MESH
NT = (((1,), (1,)), ((), ()))
HIGH = lax.Precision.HIGHEST


def cut_rows(rows, pieces):
    grains = rows // GRAIN
    pieces = min(pieces, grains)
    tail = max(1, grains // 6) if pieces > 1 else grains
    rest = grains - tail
    cuts, at = [], 0
    for i in range(pieces - 1):
        take = -(-rest // (pieces - 1 - i))
        cuts.append((at * GRAIN, take * GRAIN))
        at += take
        rest -= take
    cuts.append((at * GRAIN, tail * GRAIN))
    return cuts


def kernel(
    dims,
    anc_ref,
    x_ref,
    scale_ref,
    shift_ref,
    wconv_hbm,
    wqkv_hbm,
    wout_hbm,
    out_ref,
    wz,
    wt,
    wbuf,
    wd,
    wqkv,
    wpad,
    wkvt,
    wout,
    lat,
    act,
    yt,
    field,
    chunk,
    rt,
    nt,
    kvt,
    att,
    blk,
    blocks,
    stat_own,
    stats,
    load_sem,
    ws,
    wr,
    ss,
    sr,
    up1,
    down1,
    ys1,
    rv1,
    up2,
    down2,
    ys2,
    rv2,
    ps,
    pr,
):
    rows_here, width, chans, ranks, particles, share, aligned = dims
    tokens = rows_here * width
    total = tokens * ranks
    outer = ranks // INNER
    groups = particles // CORES
    cs = chans // ranks
    csp = chunk.shape[0]
    cpad = ranks * csp
    per_group = chans // GROUPS
    count = total * per_group
    head_dim = chans // HEADS
    tiles = chans // LANES
    bf16, f32 = jnp.bfloat16, jnp.float32
    me = lax.axis_index("rows")
    mine = lax.axis_index("particle")
    a = lax.div(me, INNER)
    b = lax.rem(me, INNER)
    other = a * INNER + (1 - b)
    grp = lax.div(mine, CORES)
    core = lax.rem(mine, CORES)

    if aligned:
        skip = lax.rem(me * share, LANES)
        conv_in = wz.at[pl.ds(pl.multiple_of(skip, GRAIN), share)]
    else:
        conv_in = wz
    qkv_in = wqkv if cpad == chans else wpad
    loads = [
        pltpu.make_async_copy(wconv_hbm, conv_in, load_sem.at[0]),
        pltpu.make_async_copy(wqkv_hbm, qkv_in, load_sem.at[1]),
        pltpu.make_async_copy(wout_hbm, wout, load_sem.at[2]),
    ]
    for load in loads:
        load.start()

    barrier = pltpu.get_barrier_semaphore()
    for k in range(1, ranks):
        pl.semaphore_signal(
            barrier, inc=1, device_id={"rows": lax.rem(me + k, ranks)}, device_id_type=MESH
        )
    for k in range(1, particles):
        pl.semaphore_signal(
            barrier,
            inc=1,
            device_id={"particle": lax.rem(mine + k, particles)},
            device_id_type=MESH,
        )

    if aligned:
        lowest = min(share * r % LANES for r in range(ranks))
        highest = max(share * r % LANES for r in range(ranks))
        for i in range(wz.shape[0] // GRAIN):
            if i * GRAIN >= highest and (i + 1) * GRAIN <= lowest + share:
                continue

            @pl.when((skip > i * GRAIN) | (skip + share <= i * GRAIN))
            def _():
                wz[i * GRAIN : (i + 1) * GRAIN] = jnp.zeros((GRAIN, chans), bf16)

    chan_r = lax.broadcasted_iota(jnp.int32, (chans, LANES), 0)
    group_r = lax.broadcasted_iota(jnp.int32, (chans, LANES), 1) * per_group
    inside = (chan_r >= group_r) & (chan_r < group_r + per_group)
    to_group = jnp.where(inside, 1.0, 0.0).astype(f32)
    group_c = lax.broadcasted_iota(jnp.int32, (LANES, chans), 0) * per_group
    chan_c = lax.broadcasted_iota(jnp.int32, (LANES, chans), 1)
    inside = (chan_c >= group_c) & (chan_c < group_c + per_group)
    to_chan = jnp.where(inside, 1.0, 0.0).astype(f32)

    x32 = x_ref[...].astype(f32)
    sums = jnp.concatenate(
        [
            jnp.sum(x32, axis=0, keepdims=True),
            jnp.sum(x32 * x32, axis=0, keepdims=True),
            jnp.zeros((6, chans), f32),
        ],
        axis=0,
    )
    stat_own[...] = jnp.dot(sums, to_group, precision=HIGH, preferred_element_type=f32)
    stats[me] = stat_own[...]

    with jax.named_scope("barrier"):
        pl.semaphore_wait(barrier, ranks + particles - 2)

    def remote(src, dst, send, recv, where):
        return pltpu.make_async_remote_copy(
            src_ref=src,
            dst_ref=dst,
            send_sem=send,
            recv_sem=recv,
            device_id=where,
            device_id_type=MESH,
        )

    class Gather:
        def __init__(self, src, buf, rows, cuts, up, down, across, rv):
            self.src, self.buf, self.rows, self.cuts = src, buf, rows, cuts
            self.up, self.down, self.across, self.rv = up, down, across, rv
            self.last = len(cuts) - 1

        def part(self, slot, i):
            start, size = self.cuts[i]
            return self.buf.at[pl.ds(pl.multiple_of(slot * self.rows + start, GRAIN), size)]

        def copy(self, slot, i, sems, row, own=False):
            start, size = self.cuts[i]
            here = self.src.at[pl.ds(start, size)] if own else self.part(slot, i)
            return remote(
                here, self.part(slot, i), sems.at[slot, i], self.rv.at[slot, i], {"rows": row}
            )

        def both(self, slot, i, do, own=False):
            @pl.when(a + 1 < outer)
            def _():
                do(self.copy(slot, i, self.up, (a + 1) * INNER + b, own))

            @pl.when(a > 0)
            def _():
                do(self.copy(slot, i, self.down, (a - 1) * INNER + b, own))

        def arrived(self, slot, i):
            self.copy(slot, i, self.across, other).wait_recv()

        def sides(self, t):
            return (
                (a >= t, a - t, a + 1 < outer, self.up, a + 1),
                (a + t < outer, a + t, a > 0, self.down, a - 1),
            )

        def begin(self):
            for i in [self.last] + list(range(self.last)):
                self.copy(me, i, self.across, other, True).start()
                self.both(me, i, lambda c: c.start(), True)
            self.buf[pl.ds(pl.multiple_of(me * self.rows, GRAIN), self.rows)] = self.src[...]

        def turn(self):
            self.arrived(other, self.last)
            self.both(other, self.last, lambda c: c.start())

        def step(self, t):
            for i in range(self.last + 1):
                for present, origin, onward, sems, target in self.sides(t):
                    near = origin * INNER + b

                    @pl.when(present)
                    def _():
                        self.arrived(near, i)

                    @pl.when(present & onward)
                    def _():
                        self.copy(near, i, sems, target * INNER + b).start()

                    if i < self.last:

                        @pl.when(present)
                        def _():
                            self.copy(near, i, self.across, other).start()

            for present, origin, onward, sems, target in self.sides(t):
                far = origin * INNER + (1 - b)

                @pl.when(present)
                def _():
                    self.arrived(far, self.last)

                @pl.when(present & onward)
                def _():
                    self.copy(far, self.last, sems, target * INNER + b).start()

        def rest(self, t):
            for present, origin, _, _, _ in self.sides(t) if t else ((None, a, 0, 0, 0),):
                far = origin * INNER + (1 - b)
                for i in range(self.last):
                    if present is None:
                        self.arrived(far, i)
                    else:

                        @pl.when(present)
                        def _():
                            self.arrived(far, i)

        def finish(self):
            def done(c):
                c.wait_send()

            for i in range(self.last + 1):
                self.copy(me, i, self.across, other, True).wait_send()
                self.both(me, i, done, True)
            self.both(other, self.last, done)
            for t in range(1, outer):
                for present, origin, onward, sems, target in self.sides(t):
                    near = origin * INNER + b
                    far = origin * INNER + (1 - b)

                    @pl.when(present & onward)
                    def _():
                        for i in range(self.last + 1):
                            self.copy(near, i, sems, target * INNER + b).wait_send()
                        self.copy(far, self.last, sems, target * INNER + b).wait_send()

                    @pl.when(present)
                    def _():
                        for i in range(self.last):
                            self.copy(near, i, self.across, other).wait_send()

    def each_slot(t, fn):
        if t == 0:
            fn(me)
            fn(other)
            return
        for present, origin in ((a >= t, a - t), (a + t < outer, a + t)):

            @pl.when(present)
            def _():
                fn(origin * INNER + b)
                fn(origin * INNER + (1 - b))

    first = Gather(x_ref, lat, tokens, cut_rows(tokens, dims_pieces(outer)), up1, down1, ys1, rv1)
    second = Gather(chunk, rt, csp, cut_rows(csp, dims_pieces(outer)), up2, down2, ys2, rv2)

    def stat_copy(k):
        return remote(
            stat_own, stats.at[me], ss.at[k - 1], sr.at[me], {"rows": lax.rem(me + k, ranks)}
        )

    def stat_from(k):
        row = lax.rem(me + ranks - k, ranks)
        return remote(stat_own, stats.at[row], ss.at[k - 1], sr.at[row], {"rows": row})

    def w_copy(k):
        dest = lax.rem(me + k, ranks)
        return remote(wt.at[dest], wbuf.at[me], ws.at[k - 1, 0], wr.at[me], {"rows": dest})

    def w_slot(k):
        return lax.rem(me + ranks - k, ranks)

    def w_pass_on(k, j, where):
        slot = w_slot(k)
        return remote(wbuf.at[slot], wbuf.at[slot], ws.at[k - 1, j], wr.at[slot], where)

    def w_arrived(k):
        w_pass_on(k, 1, {"rows": other}).wait_recv()

    def w_to_core(k):
        return w_pass_on(k, 1, {"particle": grp * CORES + (1 - core)})

    def w_to_group(k, g):
        return w_pass_on(k, 1 + g, {"particle": lax.rem(grp + g, groups) * CORES + core})

    with jax.named_scope("start"):
        first.begin()
        for k in range(1, ranks):
            stat_copy(k).start()
        loads[0].wait()
        turned = wz[...].T
        for d in range(ranks):
            wt[d, 0:cs] = turned[d * cs : (d + 1) * cs]
            if csp != cs:
                wt[d, cs:csp] = jnp.zeros((csp - cs, wt.shape[2]), bf16)
        for k in range(1, ranks):

            @pl.when(mine == k % particles)
            def _():
                w_copy(k).start()

        wbuf[me] = wt[me]
        first.turn()

    def w_forward(k):
        q = k % particles

        @pl.when(mine == q)
        def _():
            w_arrived(k)
            for g in range(1, groups):
                w_to_group(k, g).start()
            w_to_core(k).start()

    def w_relay(k):
        q = k % particles

        @pl.when((core == q % CORES) & (grp != q // CORES))
        def _():
            w_arrived(k)
            w_to_core(k).start()

    def w_last(k):
        q = k % particles

        @pl.when(core != q % CORES)
        def _():
            w_arrived(k)

    with jax.named_scope("stats"):
        for k in range(1, ranks):
            stat_from(k).wait_recv()
        by_group = jnp.sum(stats[...], axis=0) / count
        mean_g = by_group[0:1]
        inverse = lax.rsqrt(by_group[1:2] - mean_g * mean_g + 1e-05)
        back = jnp.concatenate([mean_g, inverse, jnp.zeros((6, LANES), f32)], axis=0)
        spread = jnp.dot(back, to_chan, precision=HIGH, preferred_element_type=f32)
        mean_c, inverse_c = spread[0:1], spread[1:2]
        gain = 1.0 + scale_ref[...].reshape(1, chans)
        bias = shift_ref[...].reshape(1, chans)

    def activate(slot):
        at = pl.ds(pl.multiple_of(slot * tokens, GRAIN), tokens)
        v = lat[at].astype(f32)
        v = (v - mean_c) * inverse_c * gain + bias
        act[at] = (v / (1.0 + jnp.exp(-v))).astype(bf16)

    half = total // 2
    near_half = outer // 2
    mine_half = lax.div(a, near_half)

    def conv(which):
        at = pl.multiple_of(which * half, LANES)
        yt[:, pl.ds(at, half)] = lax.dot_general(
            wd[...], act[pl.ds(at, half)], NT, preferred_element_type=f32
        )

    with jax.named_scope("g1a"):
        for t in range(1, near_half):
            first.step(t)
    with jax.named_scope("w1"):
        for k in range(1, ranks):
            w_forward(k)
    with jax.named_scope("g1b"):
        for t in range(near_half, outer):
            first.step(t)
    with jax.named_scope("w2"):
        for k in range(1, ranks):
            w_relay(k)
    with jax.named_scope("act1"):
        activate(me)
        first.rest(0)
        activate(other)
        for t in range(1, outer):
            first.rest(t)
            each_slot(t, activate)
    with jax.named_scope("w3"):
        for k in range(1, ranks):
            w_last(k)
    with jax.named_scope("wd"):
        for tap in range(TAPS):
            for j in range(tiles):
                tile = tap * tiles + j
                part = None
                for r in range(ranks):
                    if share * r < LANES * (tile + 1) and share * (r + 1) > LANES * tile:
                        i = tile - share * r // LANES
                        piece = wbuf[r, :, i * LANES : (i + 1) * LANES]
                        part = piece if part is None else part + piece
                wd[tap * csp : (tap + 1) * csp, j * LANES : (j + 1) * LANES] = part
    with jax.named_scope("conv"):
        pick = lax.broadcasted_iota(jnp.int32, (csp, chans), 0)
        at = lax.broadcasted_iota(jnp.int32, (csp, chans), 1)
        pick = jnp.where((at == me * cs + pick) & (pick < cs), 1.0, 0.0).astype(bf16)
        field[...] = lax.dot_general(pick, lat[...], NT, preferred_element_type=f32)
        conv(mine_half)
        conv(1 - mine_half)

    with jax.named_scope("taps"):
        lane = lax.broadcasted_iota(jnp.int32, (1, total), 1)
        column = lax.rem(lane, width)
        has_left = column > 0
        has_right = column < width - 1
        has_above = lane >= width
        has_below = lane < total - width

        def add_taps(i, carry):
            def tap(row, col):
                base = (row * 3 + col) * csp
                return yt[pl.ds(pl.multiple_of(base + i * GRAIN, GRAIN), GRAIN), :]

            cols = []
            for col in range(3):
                above = jnp.where(has_above, pltpu.roll(tap(0, col), width, 1), 0.0)
                below = jnp.where(has_below, pltpu.roll(tap(2, col), total - width, 1), 0.0)
                cols.append(tap(1, col) + above + below)
            left = jnp.where(has_left, pltpu.roll(cols[0], 1, 1), 0.0)
            right = jnp.where(has_right, pltpu.roll(cols[2], total - 1, 1), 0.0)
            at = pl.ds(pl.multiple_of(i * GRAIN, GRAIN), GRAIN)
            chunk[at] = (field[at] + (cols[1] + left + right)).astype(bf16)
            return carry

        lax.fori_loop(0, csp // GRAIN, add_taps, 0)

    own_r = lax.broadcasted_iota(jnp.int32, (csp, csp), 0)
    own_c = lax.broadcasted_iota(jnp.int32, (csp, csp), 1)
    same = (lax.div(own_r, per_group) == lax.div(own_c, per_group)) & (own_r < cs) & (own_c < cs)
    same = jnp.where(same, 1.0, 0.0).astype(f32)
    lane = lax.broadcasted_iota(jnp.int32, (csp, LANES), 1)

    def normalize(slot):
        at = pl.ds(pl.multiple_of(slot * csp, GRAIN), csp)
        v = rt[at].astype(f32)
        both = jnp.where(
            lane == 0,
            jnp.sum(v, axis=1, keepdims=True),
            jnp.where(lane == 1, jnp.sum(v * v, axis=1, keepdims=True), 0.0),
        )
        both = jnp.dot(same, both, precision=HIGH, preferred_element_type=f32) / count
        mean = both[:, 0:1]
        inv = lax.rsqrt(both[:, 1:2] - mean * mean + 1e-05)
        nt[at] = ((v - mean) * inv).astype(bf16)

    with jax.named_scope("g2"):
        second.begin()
        loads[1].wait()
        if cpad != chans:
            wqkv[...] = jnp.zeros_like(wqkv)
            for d in range(ranks):
                wqkv[d * csp : d * csp + cs] = wpad[d * cs : (d + 1) * cs]
        for n in range(2 * tiles):
            wkvt[n * LANES : (n + 1) * LANES] = wqkv[
                :, chans + n * LANES : chans + (n + 1) * LANES
            ].T
        second.turn()
        normalize(me)
        for t in range(1, outer):
            second.step(t)
        second.rest(0)
        normalize(other)
        for t in range(1, outer):
            second.rest(t)
            each_slot(t, normalize)

    with jax.named_scope("qkv"):
        step = 2 * LANES
        for n in range(2 * chans // step):
            kvt[n * step : (n + 1) * step] = jnp.dot(
                wkvt[n * step : (n + 1) * step], nt[...], preferred_element_type=f32
            ).astype(bf16)
        row = lax.broadcasted_iota(jnp.int32, (tokens, total), 0)
        at = lax.broadcasted_iota(jnp.int32, (tokens, total), 1)
        pick = jnp.where(at == me * tokens + row, 1.0, 0.0).astype(bf16)
        mine_n = lax.dot_general(pick, nt[...], NT, preferred_element_type=f32).astype(bf16)
        resid = lax.dot_general(pick, rt[...], NT, preferred_element_type=f32)
        if cpad != chans:
            resid = jnp.concatenate(
                [resid[:, d * csp : d * csp + cs] for d in range(ranks)], axis=1
            )
        query = jnp.dot(mine_n, wqkv[:, :chans], preferred_element_type=f32).astype(bf16)

    with jax.named_scope("attn"):
        pair = 2 * head_dim
        lane = lax.broadcasted_iota(jnp.int32, (tokens, pair), 1)
        low = lane < head_dim
        zero = jnp.zeros((tokens, pair), bf16)
        for h in range(HEADS // 2):
            q = query[:, h * pair : (h + 1) * pair]
            q = jnp.concatenate([jnp.where(low, q, zero), jnp.where(low, zero, q)], axis=0)
            scores = jnp.dot(
                q, kvt[h * pair : (h + 1) * pair], preferred_element_type=f32
            ) * (head_dim ** (-0.5))
            top = jnp.max(scores, axis=1, keepdims=True)
            weights = jnp.exp(scores - top)
            norm = jnp.sum(weights, axis=1, keepdims=True)
            mixed = (
                lax.dot_general(
                    weights.astype(bf16),
                    kvt[chans + h * pair : chans + (h + 1) * pair],
                    NT,
                    preferred_element_type=f32,
                )
                / norm
            )
            att[:, h * pair : (h + 1) * pair] = jnp.where(
                low, mixed[:tokens], mixed[tokens:]
            ).astype(bf16)
    with jax.named_scope("proj"):
        loads[2].wait()
        block = (resid + jnp.dot(att[...], wout[...], preferred_element_type=f32)).astype(bf16)
        blk[...] = block
        blocks[mine] = block

    def to_particle(k):
        peer = lax.rem(mine + k, particles)
        return remote(blk, blocks.at[mine], ps.at[k - 1], pr.at[k - 1], {"particle": peer})

    with jax.named_scope("resample"):
        for k in range(1, particles):
            to_particle(k).start()
        for k in range(1, particles):
            to_particle(k).wait_recv()
        out_ref[...] = blocks[anc_ref[mine]]
    with jax.named_scope("drain"):
        for k in range(1, particles):
            to_particle(k).wait_send()
        first.finish()
        second.finish()
        for k in range(1, ranks):
            stat_copy(k).wait_send()
            q = k % particles

            @pl.when(mine == q)
            def _():
                w_copy(k).wait_send()
                for g in range(1, groups):
                    w_to_group(k, g).wait_send()

            @pl.when(core == q % CORES)
            def _():
                w_to_core(k).wait_send()


def dims_pieces(outer):
    return 3 if outer <= 4 else 2


def per_device(latent, ada_scale, ada_shift, conv_weight, qkv_weight, out_weight, ancestors):
    _, rows_here, width, chans = latent.shape
    tokens = rows_here * width
    ranks = lax.axis_size("rows")
    particles = lax.axis_size("particle")
    groups = particles // CORES
    total = tokens * ranks
    share = conv_weight.shape[0]
    span = max(-(-(share * r % LANES + share) // LANES) for r in range(ranks)) * LANES
    aligned = math.gcd(share, LANES) % GRAIN == 0
    if not aligned:
        start = lax.rem(lax.axis_index("rows") * share, LANES)
        conv_weight = lax.dynamic_update_slice(
            jnp.zeros((span, chans), conv_weight.dtype), conv_weight, (start, 0)
        )
    cs = chans // ranks
    csp = -(-cs // GRAIN) * GRAIN
    cpad = csp * ranks
    pieces = dims_pieces(ranks // INNER)
    n1 = len(cut_rows(tokens, pieces))
    n2 = len(cut_rows(csp, pieces))
    dims = (rows_here, width, chans, ranks, particles, share, aligned)
    bf16, f32 = jnp.bfloat16, jnp.float32
    dma = pltpu.SemaphoreType.DMA
    out = pl.pallas_call(
        functools.partial(kernel, dims),
        out_shape=jax.ShapeDtypeStruct((tokens, chans), bf16),
        in_specs=[pl.BlockSpec(memory_space=pltpu.SMEM)]
        + [pl.BlockSpec(memory_space=pltpu.VMEM)] * 3
        + [pl.BlockSpec(memory_space=pl.ANY)] * 3,
        out_specs=pl.BlockSpec(memory_space=pltpu.VMEM),
        scratch_shapes=[
            pltpu.VMEM((span, chans), bf16),
            pltpu.VMEM((ranks, csp, span), bf16),
            pltpu.VMEM((ranks, csp, span), bf16),
            pltpu.VMEM((TAPS * csp, chans), bf16),
            pltpu.VMEM((cpad, 3 * chans), bf16),
            pltpu.VMEM((GRAIN, LANES) if cpad == chans else qkv_weight.shape, bf16),
            pltpu.VMEM((2 * chans, cpad), bf16),
            pltpu.VMEM(out_weight.shape, bf16),
            pltpu.VMEM((total, chans), bf16),
            pltpu.VMEM((total, chans), bf16),
            pltpu.VMEM((TAPS * csp, total), f32),
            pltpu.VMEM((csp, total), f32),
            pltpu.VMEM((csp, total), bf16),
            pltpu.VMEM((cpad, total), bf16),
            pltpu.VMEM((cpad, total), bf16),
            pltpu.VMEM((2 * chans, total), bf16),
            pltpu.VMEM((tokens, chans), bf16),
            pltpu.VMEM((tokens, chans), bf16),
            pltpu.VMEM((particles, tokens, chans), bf16),
            pltpu.VMEM((8, LANES), f32),
            pltpu.VMEM((ranks, 8, LANES), f32),
            dma((3,)),
            dma((ranks, 1 + groups)),
            dma((ranks,)),
            dma((ranks,)),
            dma((ranks,)),
            dma((ranks, n1)),
            dma((ranks, n1)),
            dma((ranks, n1)),
            dma((ranks, n1)),
            dma((ranks, n2)),
            dma((ranks, n2)),
            dma((ranks, n2)),
            dma((ranks, n2)),
            dma((particles,)),
            dma((particles,)),
        ],
        compiler_params=pltpu.CompilerParams(
            collective_id=0, has_side_effects=True, vmem_limit_bytes=64000 * 1024
        ),
        name="block",
    )(
        ancestors,
        latent.reshape(tokens, chans),
        ada_scale,
        ada_shift,
        conv_weight,
        qkv_weight,
        out_weight,
    )
    return out.reshape(latent.shape)


def solution(mesh):
    in_specs = (P("particle", "rows", None, None), P(), P(), P("rows", None), P(), P(), P())
    out_specs = P("particle", "rows", None, None)
    return jax.shard_map(
        per_device, mesh=mesh, in_specs=in_specs, out_specs=out_specs, check_vma=False
    )
```

time: 66.2 us -> 57.8 us (0.87)
  Pallas kernels: 63.9 us -> 55.7 us
    pallas_call x1, Pallas kernels: 63.9 us -> 55.7 us  [per_device(): pl.pallas_call(functools.partial(kernel, dims), out_shape=jax.ShapeDtypeS...]
where the time goes in v1:
time: 57.8 us; the launch traced here: 57.3 us
  Pallas kernels  55.7 us (96%)
  local copies, waits for them, and re-layouts  1.56 us (3%)
    pallas_call x1, Pallas kernels, per_device(): pl.pallas_call(functools.partial(kernel, dims), out_shape=jax.ShapeDtypeS...  55.7 us
    unnamed x1, local copies, waits for them, and re-layouts  1.56 us

profile of v1, /device:TPU:0, one launch (start us, length us, event | category | flops | bytes accessed | tf_op | source)
XLA Modules:
  0.0 57.3 jit_solution(1059104179219679215)
XLA Ops:
  0.0 55.7 %block.1 = bf16[96,640]{1,0:T(8,128)(2,1)} custom-call(s32[4]{0:T(128)} %anc_ref.1, bf16[96,640]{1,0:T(8,128)(2,1)} %bitcast.3, f32[640]{0:T(1024)} %scale_ref.1, f32[640]{0:T(1024)} %shift_ref.1, bf16[720,640]{1,0:T(8,128)(2,1)} %wconv_hbm.1, bf16[640,1920]{1,0:T(8,128)(2,1)} %wqkv_hbm.1, bf16[640,640]{1,0:T(8,128)(2,1)} %wout_hbm.1), custom_call_target="tpu_custom_call" | custom-call | tf_op jit(solution)/shard_map/block/pallas_call | solution.py:619
  55.7 1.6 %copy.9 = bf16[1,4,24,640]{3,2,1,0:T(8,128)(2,1)} copy(bf16[1,4,24,640]{3,2,1,0:T(8,128)(2,1)} %bitcast.2) | data formatting | bytes 245760

commit v2 on v1

v2 whole, which is shorter than its diff:
```python
import functools
import math

import jax
import jax.numpy as jnp
from jax import lax
from jax.experimental import pallas as pl
from jax.experimental.pallas import tpu as pltpu
from jax.sharding import PartitionSpec as P

HEADS = 10
GROUPS = 32
INNER = 2
CUT1 = 2
CUT2 = 1
CORES = 2
LANES = 128
GRAIN = 16
TAPS = 9
MESH = pl.DeviceIdType.MESH
NT = (((1,), (1,)), ((), ()))
HIGH = lax.Precision.HIGHEST


def cut_rows(rows, grains):
    step = grains * GRAIN
    return [(at, min(step, rows - at)) for at in range(0, rows, step)]


def kernel(
    dims,
    anc_ref,
    x_hbm,
    scale_hbm,
    shift_hbm,
    wconv_hbm,
    wqkv_hbm,
    wout_hbm,
    out_ref,
    x_ref,
    scale_ref,
    shift_ref,
    wz,
    wt,
    wbuf,
    wd,
    wqkv,
    wpad,
    wkvt,
    wout,
    lat,
    act,
    yt,
    field,
    chunk,
    rt,
    nt,
    kvt,
    att,
    blocks,
    stat_own,
    stats,
    load_sem,
    ws,
    wr,
    ss,
    sent1,
    near1,
    far1,
    sent2,
    near2,
    far2,
    ps,
    pr,
):
    rows_here, width, chans, ranks, particles, share = dims
    tokens = rows_here * width
    total = tokens * ranks
    outer = ranks // INNER
    groups = particles // CORES
    cs = chans // ranks
    csp = chunk.shape[0]
    cpad = ranks * csp
    per_group = chans // GROUPS
    count = total * per_group
    head_dim = chans // HEADS
    tiles = chans // LANES
    bf16, f32 = jnp.bfloat16, jnp.float32
    me = lax.axis_index("rows")
    mine = lax.axis_index("particle")
    a = lax.div(me, INNER)
    b = lax.rem(me, INNER)
    other = a * INNER + (1 - b)
    grp = lax.div(mine, CORES)
    core = lax.rem(mine, CORES)

    conv_in = wz.at[0 : wconv_hbm.shape[0]]
    qkv_in = wqkv if cpad == chans else wpad
    loads = [
        pltpu.make_async_copy(wconv_hbm, conv_in, load_sem.at[0]),
        pltpu.make_async_copy(wqkv_hbm, qkv_in, load_sem.at[1]),
        pltpu.make_async_copy(wout_hbm, wout, load_sem.at[2]),
        pltpu.make_async_copy(x_hbm, x_ref, load_sem.at[3]),
        pltpu.make_async_copy(scale_hbm, scale_ref, load_sem.at[4]),
        pltpu.make_async_copy(shift_hbm, shift_ref, load_sem.at[5]),
    ]
    for i in (3, 0, 4, 5, 1, 2):
        loads[i].start()

    barrier = pltpu.get_barrier_semaphore()
    for k in range(1, ranks):
        pl.semaphore_signal(
            barrier, inc=1, device_id={"rows": lax.rem(me + k, ranks)}, device_id_type=MESH
        )
    for k in range(1, particles):
        pl.semaphore_signal(
            barrier,
            inc=1,
            device_id={"particle": lax.rem(mine + k, particles)},
            device_id_type=MESH,
        )

    if wz.shape[0] > wconv_hbm.shape[0]:
        tail = wz.shape[0] - wconv_hbm.shape[0]
        wz[wconv_hbm.shape[0] :] = jnp.zeros((tail, chans), bf16)

    chan_r = lax.broadcasted_iota(jnp.int32, (chans, LANES), 0)
    group_r = lax.broadcasted_iota(jnp.int32, (chans, LANES), 1) * per_group
    inside = (chan_r >= group_r) & (chan_r < group_r + per_group)
    to_group = jnp.where(inside, 1.0, 0.0).astype(f32)
    group_c = lax.broadcasted_iota(jnp.int32, (LANES, chans), 0) * per_group
    chan_c = lax.broadcasted_iota(jnp.int32, (LANES, chans), 1)
    inside = (chan_c >= group_c) & (chan_c < group_c + per_group)
    to_chan = jnp.where(inside, 1.0, 0.0).astype(f32)

    loads[3].wait()
    x32 = x_ref[...].astype(f32)
    sums = jnp.concatenate(
        [
            jnp.sum(x32, axis=0, keepdims=True),
            jnp.sum(x32 * x32, axis=0, keepdims=True),
            jnp.zeros((6, chans), f32),
        ],
        axis=0,
    )
    stat_own[...] = jnp.dot(sums, to_group, precision=HIGH, preferred_element_type=f32)
    stats[me] = stat_own[...]

    with jax.named_scope("turn"):
        loads[0].wait()
        turned = wz[...].T
        for d in range(ranks):
            wt[d, 0:cs] = turned[d * cs : (d + 1) * cs]
            if csp != cs:
                wt[d, cs:csp] = jnp.zeros((csp - cs, wt.shape[2]), bf16)

    with jax.named_scope("barrier"):
        pl.semaphore_wait(barrier, ranks + particles - 2)

    def remote(src, dst, send, recv, where):
        return pltpu.make_async_remote_copy(
            src_ref=src,
            dst_ref=dst,
            send_sem=send,
            recv_sem=recv,
            device_id=where,
            device_id_type=MESH,
        )

    class Gather:
        def __init__(self, src, buf, rows, cuts, sent, near, far):
            self.src, self.buf, self.rows, self.cuts = src, buf, rows, cuts
            self.sent, self.near, self.far = sent, near, far
            self.pieces = range(len(cuts))

        def rows_of(self, slot, start, size):
            return self.buf.at[pl.ds(pl.multiple_of(slot * self.rows + start, GRAIN), size)]

        def onto(self, origin, i, side, own=False):
            start, size = self.cuts[i]
            dst = self.rows_of(origin * INNER + b, start, size)
            src = self.src.at[pl.ds(start, size)] if own else dst
            recv = self.near.at[origin, i] if side else self.far.at[origin]
            row = (a + side) * INNER + b if side else other
            return remote(src, dst, self.sent.at[side + 1], recv, {"rows": row})

        def pass_on(self, origin, i, side, own=False):
            onward = (a + 1 < outer) if side == 1 else (a > 0)

            @pl.when(onward)
            def _():
                self.onto(origin, i, side, own).start()

        def begin(self, pieces):
            for i in pieces:
                self.onto(a, i, 0, True).start()
                self.pass_on(a, i, 1, True)
                self.pass_on(a, i, -1, True)

        def keep(self):
            self.buf[pl.ds(pl.multiple_of(me * self.rows, GRAIN), self.rows)] = self.src[...]

        def step(self, t):
            for i in self.pieces:
                for present, origin, side in ((a >= t, a - t, 1), (a + t < outer, a + t, -1)):

                    @pl.when(present)
                    def _():
                        self.onto(origin, i, 1).wait_recv()
                        self.pass_on(origin, i, side)
                        self.onto(origin, i, 0).start()

        def far_slab(self, origin):
            slab = self.rows_of(origin * INNER + (1 - b), 0, self.rows)
            remote(slab, slab, self.sent.at[1], self.far.at[origin], {"rows": other}).wait_recv()

        def rest(self, t):
            if t == 0:
                self.far_slab(a)
                return
            for present, origin in ((a >= t, a - t), (a + t < outer, a + t)):

                @pl.when(present)
                def _():
                    self.far_slab(origin)

        def sent_all(self, side, slabs):
            part = self.buf.at[0 : slabs * self.rows]
            remote(part, part, self.sent.at[side + 1], self.far.at[0], {"rows": other}).wait_send()

        def finish(self):
            self.sent_all(0, outer)
            for v in range(outer):

                @pl.when(a == v)
                def _():
                    if v + 1 < outer:
                        self.sent_all(1, v + 1)
                    if v > 0:
                        self.sent_all(-1, outer - v)

    def each_slot(t, fn):
        if t == 0:
            fn(me)
            fn(other)
            return
        for present, origin in ((a >= t, a - t), (a + t < outer, a + t)):

            @pl.when(present)
            def _():
                fn(origin * INNER + b)
                fn(origin * INNER + (1 - b))

    near_half = outer // 2
    first = Gather(x_ref, lat, tokens, cut_rows(tokens, CUT1), sent1, near1, far1)
    second = Gather(chunk, rt, csp, cut_rows(csp, CUT2), sent2, near2, far2)

    def stat_copy(k):
        return remote(
            stat_own, stats.at[me], ss.at[0], ss.at[1], {"rows": lax.rem(me + k, ranks)}
        )

    def stat_all():
        part = stats.at[0 : ranks - 1]
        return remote(part, part, ss.at[0], ss.at[1], {"rows": other})

    def w_copy(k):
        dest = lax.rem(me + k, ranks)
        return remote(wt.at[dest], wbuf.at[me], ws.at[0], wr.at[me], {"rows": dest})

    def w_slot(k):
        return lax.rem(me + ranks - k, ranks)

    def w_pass_on(k, j, where):
        slot = w_slot(k)
        return remote(wbuf.at[slot], wbuf.at[slot], ws.at[j], wr.at[slot], where)

    def w_arrived(k):
        w_pass_on(k, 1, {"rows": other}).wait_recv()

    def w_to_core(k):
        return w_pass_on(k, 1, {"particle": grp * CORES + (1 - core)})

    def w_to_group(k, g):
        return w_pass_on(k, 1 + g, {"particle": lax.rem(grp + g, groups) * CORES + core})

    with jax.named_scope("start"):
        for k in range(1, ranks):
            stat_copy(k).start()
        for k in range(1, ranks):

            @pl.when(mine == k % particles)
            def _():
                w_copy(k).start()

        first.begin(first.pieces)
        first.keep()
        wbuf[me] = wt[me]

    def w_forward(k):
        q = k % particles

        @pl.when(mine == q)
        def _():
            w_arrived(k)
            for g in range(1, groups):
                w_to_group(k, g).start()
            w_to_core(k).start()

    def w_relay(k):
        q = k % particles

        @pl.when((core == q % CORES) & (grp != q // CORES))
        def _():
            w_arrived(k)
            w_to_core(k).start()

    def w_last(k):
        q = k % particles

        @pl.when(core != q % CORES)
        def _():
            w_arrived(k)

    with jax.named_scope("w1"):
        for k in range(1, ranks):
            w_forward(k)
    with jax.named_scope("g1a"):
        for t in range(1, near_half):
            first.step(t)
    with jax.named_scope("stats"):
        stat_all().wait_recv()
        by_group = jnp.sum(stats[...], axis=0) / count
        mean_g = by_group[0:1]
        inverse = lax.rsqrt(by_group[1:2] - mean_g * mean_g + 1e-05)
        back = jnp.concatenate([mean_g, inverse, jnp.zeros((6, LANES), f32)], axis=0)
        spread = jnp.dot(back, to_chan, precision=HIGH, preferred_element_type=f32)
        mean_c, inverse_c = spread[0:1], spread[1:2]
        loads[4].wait()
        loads[5].wait()
        gain = 1.0 + scale_ref[...].reshape(1, chans)
        bias = shift_ref[...].reshape(1, chans)

    def activate(slot):
        at = pl.ds(pl.multiple_of(slot * tokens, GRAIN), tokens)
        v = lat[at].astype(f32)
        v = (v - mean_c) * inverse_c * gain + bias
        act[at] = (v / (1.0 + jnp.exp(-v))).astype(bf16)

    half = total // 2
    mine_half = lax.div(a, near_half)

    def conv(which):
        at = pl.multiple_of(which * half, LANES)
        yt[:, pl.ds(at, half)] = lax.dot_general(
            wd[...], act[pl.ds(at, half)], NT, preferred_element_type=f32
        )

    with jax.named_scope("own"):
        activate(me)
    with jax.named_scope("g1b"):
        for t in range(near_half, outer - 1):
            first.step(t)
    with jax.named_scope("w2"):
        for k in range(1, ranks):
            w_relay(k)
    with jax.named_scope("act1"):
        first.rest(0)
        activate(other)
        for t in range(1, near_half):
            first.rest(t)
            each_slot(t, activate)
    with jax.named_scope("g1c"):
        first.step(outer - 1)
    with jax.named_scope("act2"):
        for t in range(near_half, outer - 1):
            first.rest(t)
            each_slot(t, activate)
    with jax.named_scope("w3"):
        for k in range(1, ranks):
            w_last(k)
    with jax.named_scope("wd"):
        line = jnp.concatenate([wbuf[r][:, :share] for r in range(ranks)], axis=1)
        for tap in range(TAPS):
            wd[tap * csp : (tap + 1) * csp] = line[:, tap * chans : (tap + 1) * chans]
    with jax.named_scope("conv1"):
        conv(mine_half)
    with jax.named_scope("act3"):
        first.rest(outer - 1)
        each_slot(outer - 1, activate)
    with jax.named_scope("conv2"):
        pick = lax.broadcasted_iota(jnp.int32, (csp, chans), 0)
        at = lax.broadcasted_iota(jnp.int32, (csp, chans), 1)
        pick = jnp.where((at == me * cs + pick) & (pick < cs), 1.0, 0.0).astype(bf16)
        field[...] = lax.dot_general(pick, lat[...], NT, preferred_element_type=f32)
        conv(1 - mine_half)

    with jax.named_scope("taps"):
        lane = lax.broadcasted_iota(jnp.int32, (1, total), 1)
        column = lax.rem(lane, width)
        has_left = column > 0
        has_right = column < width - 1
        has_above = lane >= width
        has_below = lane < total - width

        def add_taps(i, carry):
            def tap(row, col):
                base = (row * 3 + col) * csp
                return yt[pl.ds(pl.multiple_of(base + i * GRAIN, GRAIN), GRAIN), :]

            cols = []
            for col in range(3):
                above = jnp.where(has_above, pltpu.roll(tap(0, col), width, 1), 0.0)
                below = jnp.where(has_below, pltpu.roll(tap(2, col), total - width, 1), 0.0)
                cols.append(tap(1, col) + above + below)
            left = jnp.where(has_left, pltpu.roll(cols[0], 1, 1), 0.0)
            right = jnp.where(has_right, pltpu.roll(cols[2], total - 1, 1), 0.0)
            at = pl.ds(pl.multiple_of(i * GRAIN, GRAIN), GRAIN)
            chunk[at] = (field[at] + (cols[1] + left + right)).astype(bf16)
            return carry

        for i in second.pieces:
            start, size = second.cuts[i]
            lax.fori_loop(start // GRAIN, (start + size) // GRAIN, add_taps, 0)
            second.begin([i])
        second.keep()

    own_r = lax.broadcasted_iota(jnp.int32, (csp, csp), 0)
    own_c = lax.broadcasted_iota(jnp.int32, (csp, csp), 1)
    same = (lax.div(own_r, per_group) == lax.div(own_c, per_group)) & (own_r < cs) & (own_c < cs)
    same = jnp.where(same, 1.0, 0.0).astype(f32)
    lane = lax.broadcasted_iota(jnp.int32, (csp, LANES), 1)

    def normalize(slot):
        at = pl.ds(pl.multiple_of(slot * csp, GRAIN), csp)
        v = rt[at].astype(f32)
        both = jnp.where(
            lane == 0,
            jnp.sum(v, axis=1, keepdims=True),
            jnp.where(lane == 1, jnp.sum(v * v, axis=1, keepdims=True), 0.0),
        )
        both = jnp.dot(same, both, precision=HIGH, preferred_element_type=f32) / count
        mean = both[:, 0:1]
        inv = lax.rsqrt(both[:, 1:2] - mean * mean + 1e-05)
        nt[at] = ((v - mean) * inv).astype(bf16)

    with jax.named_scope("g2"):
        loads[1].wait()
        if cpad != chans:
            wqkv[...] = jnp.zeros_like(wqkv)
            for d in range(ranks):
                wqkv[d * csp : d * csp + cs] = wpad[d * cs : (d + 1) * cs]
        for n in range(2 * tiles):
            wkvt[n * LANES : (n + 1) * LANES] = wqkv[
                :, chans + n * LANES : chans + (n + 1) * LANES
            ].T
        normalize(me)
        for t in range(1, outer):
            second.step(t)
        second.rest(0)
        normalize(other)
        for t in range(1, outer):
            second.rest(t)
            each_slot(t, normalize)

    with jax.named_scope("qkv"):
        step = 2 * LANES
        for n in range(2 * chans // step):
            kvt[n * step : (n + 1) * step] = jnp.dot(
                wkvt[n * step : (n + 1) * step], nt[...], preferred_element_type=f32
            ).astype(bf16)
        row = lax.broadcasted_iota(jnp.int32, (tokens, total), 0)
        at = lax.broadcasted_iota(jnp.int32, (tokens, total), 1)
        pick = jnp.where(at == me * tokens + row, 1.0, 0.0).astype(bf16)
        mine_n = lax.dot_general(pick, nt[...], NT, preferred_element_type=f32).astype(bf16)
        resid = lax.dot_general(pick, rt[...], NT, preferred_element_type=f32)
        if cpad != chans:
            resid = jnp.concatenate(
                [resid[:, d * csp : d * csp + cs] for d in range(ranks)], axis=1
            )
        query = jnp.dot(mine_n, wqkv[:, :chans], preferred_element_type=f32).astype(bf16)

    with jax.named_scope("attn"):
        pair = 2 * head_dim
        lane = lax.broadcasted_iota(jnp.int32, (tokens, pair), 1)
        low = lane < head_dim
        zero = jnp.zeros((tokens, pair), bf16)
        for h in range(HEADS // 2):
            q = query[:, h * pair : (h + 1) * pair]
            q = jnp.concatenate([jnp.where(low, q, zero), jnp.where(low, zero, q)], axis=0)
            scores = jnp.dot(
                q, kvt[h * pair : (h + 1) * pair], preferred_element_type=f32
            ) * (head_dim ** (-0.5))
            top = jnp.max(scores, axis=1, keepdims=True)
            weights = jnp.exp(scores - top)
            norm = jnp.sum(weights, axis=1, keepdims=True)
            mixed = (
                lax.dot_general(
                    weights.astype(bf16),
                    kvt[chans + h * pair : chans + (h + 1) * pair],
                    NT,
                    preferred_element_type=f32,
                )
                / norm
            )
            att[:, h * pair : (h + 1) * pair] = jnp.where(
                low, mixed[:tokens], mixed[tokens:]
            ).astype(bf16)
    def to_core(p, j):
        where = {"particle": grp * CORES + (1 - core)}
        return remote(blocks.at[p, j], blocks.at[p, j], ps.at[0], pr.at[0, 0], where)

    def to_group(j, g):
        where = {"particle": lax.rem(grp + g, groups) * CORES + core}
        return remote(blocks.at[mine, j], blocks.at[mine, j], ps.at[g], pr.at[g, j], where)

    def from_group(j, g):
        part = blocks.at[of_group(g, core), j]
        remote(part, part, ps.at[g], pr.at[g, j], {"rows": other}).wait_recv()

    def whole_blocks(n, sem):
        part = blocks.at[0:n]
        return remote(part, part, ps.at[sem], pr.at[0, 0], {"rows": other})

    def of_group(g, side):
        return lax.rem(grp + groups - g, groups) * CORES + side

    with jax.named_scope("proj"):
        loads[2].wait()
        for j in range(tiles):
            at = slice(j * LANES, (j + 1) * LANES)
            blocks[mine, j] = (
                resid[:, at] + jnp.dot(att[...], wout[:, at], preferred_element_type=f32)
            ).astype(bf16)
            for g in range(1, groups):
                to_group(j, g).start()
            to_core(mine, j).start()

    with jax.named_scope("resample"):
        for j in range(tiles):
            for g in range(1, groups):
                from_group(j, g)
                to_core(of_group(g, core), j).start()
        whole_blocks(groups, 0).wait_recv()
        for j in range(tiles):
            out_ref[:, j * LANES : (j + 1) * LANES] = blocks[anc_ref[mine], j]
    with jax.named_scope("drain"):
        whole_blocks(groups, 0).wait_send()
        for g in range(1, groups):
            whole_blocks(1, g).wait_send()
        first.finish()
        second.finish()
        stat_all().wait_send()
        for q in range(particles):
            count = len(range(q, ranks, particles)) - (q == 0)

            @pl.when(mine == q)
            def _():
                part = wbuf.at[0:count]
                for g in [0] + list(range(2, groups + 1)):
                    remote(part, part, ws.at[g], wr.at[0], {"rows": other}).wait_send()

        for c in range(CORES):
            count = sum(k % particles % CORES == c for k in range(1, ranks))

            @pl.when(core == c)
            def _():
                part = wbuf.at[0:count]
                remote(part, part, ws.at[1], wr.at[0], {"rows": other}).wait_send()


def per_device(latent, ada_scale, ada_shift, conv_weight, qkv_weight, out_weight, ancestors):
    _, rows_here, width, chans = latent.shape
    tokens = rows_here * width
    ranks = lax.axis_size("rows")
    particles = lax.axis_size("particle")
    groups = particles // CORES
    total = tokens * ranks
    share = conv_weight.shape[0]
    span = -(-share // LANES) * LANES
    if share % GRAIN:
        conv_weight = jnp.pad(conv_weight, ((0, span - share), (0, 0)))
    cs = chans // ranks
    csp = -(-cs // GRAIN) * GRAIN
    cpad = csp * ranks
    outer = ranks // INNER
    n1, n2 = len(cut_rows(tokens, CUT1)), len(cut_rows(csp, CUT2))
    dims = (rows_here, width, chans, ranks, particles, share)
    bf16, f32 = jnp.bfloat16, jnp.float32
    dma = pltpu.SemaphoreType.DMA
    out = pl.pallas_call(
        functools.partial(kernel, dims),
        out_shape=jax.ShapeDtypeStruct((tokens, chans), bf16),
        in_specs=[pl.BlockSpec(memory_space=pltpu.SMEM)]
        + [pl.BlockSpec(memory_space=pl.ANY)] * 6,
        out_specs=pl.BlockSpec(memory_space=pltpu.VMEM),
        scratch_shapes=[
            pltpu.VMEM((tokens, chans), bf16),
            pltpu.VMEM(ada_scale.shape, f32),
            pltpu.VMEM(ada_shift.shape, f32),
            pltpu.VMEM((span, chans), bf16),
            pltpu.VMEM((ranks, csp, span), bf16),
            pltpu.VMEM((ranks, csp, span), bf16),
            pltpu.VMEM((TAPS * csp, chans), bf16),
            pltpu.VMEM((cpad, 3 * chans), bf16),
            pltpu.VMEM((GRAIN, LANES) if cpad == chans else qkv_weight.shape, bf16),
            pltpu.VMEM((2 * chans, cpad), bf16),
            pltpu.VMEM(out_weight.shape, bf16),
            pltpu.VMEM((total, chans), bf16),
            pltpu.VMEM((total, chans), bf16),
            pltpu.VMEM((TAPS * csp, total), f32),
            pltpu.VMEM((csp, total), f32),
            pltpu.VMEM((csp, total), bf16),
            pltpu.VMEM((cpad, total), bf16),
            pltpu.VMEM((cpad, total), bf16),
            pltpu.VMEM((2 * chans, total), bf16),
            pltpu.VMEM((tokens, chans), bf16),
            pltpu.VMEM((particles, chans // LANES, tokens, LANES), bf16),
            pltpu.VMEM((8, LANES), f32),
            pltpu.VMEM((ranks, 8, LANES), f32),
            dma((6,)),
            dma((1 + groups,)),
            dma((ranks,)),
            dma((2,)),
            dma((3,)),
            dma((outer, n1)),
            dma((outer,)),
            dma((3,)),
            dma((outer, n2)),
            dma((outer,)),
            dma((groups,)),
            dma((groups, chans // LANES)),
        ],
        compiler_params=pltpu.CompilerParams(
            collective_id=0, has_side_effects=True, vmem_limit_bytes=64000 * 1024
        ),
        name="block",
    )(
        ancestors,
        latent.reshape(tokens, chans),
        ada_scale,
        ada_shift,
        conv_weight,
        qkv_weight,
        out_weight,
    )
    return out.reshape(latent.shape)


def solution(mesh):
    in_specs = (P("particle", "rows", None, None), P(), P(), P("rows", None), P(), P(), P())
    out_specs = P("particle", "rows", None, None)
    return jax.shard_map(
        per_device, mesh=mesh, in_specs=in_specs, out_specs=out_specs, check_vma=False
    )
```

time: 57.8 us -> 52 us (0.90)
  Pallas kernels: 55.7 us -> 50.2 us
    pallas_call x1, Pallas kernels: 55.7 us -> 50.2 us  [per_device(): pl.pallas_call(functools.partial(kernel, dims), out_shape=jax.ShapeDtypeS...]
where the time goes in v2:
time: 52 us; the launch traced here: 51.8 us
  Pallas kernels  50.2 us (97%)
  local copies, waits for them, and re-layouts  1.56 us (3%)
    pallas_call x1, Pallas kernels, per_device(): pl.pallas_call(functools.partial(kernel, dims), out_shape=jax.ShapeDtypeS...  50.2 us
    unnamed x1, local copies, waits for them, and re-layouts  1.56 us

profile of v2, /device:TPU:0, one launch (start us, length us, event | category | flops | bytes accessed | tf_op | source)
XLA Modules:
  0.0 51.8 jit_solution(4438993054236790074)
XLA Ops:
  0.0 50.2 %block.1 = bf16[96,640]{1,0:T(8,128)(2,1)} custom-call(s32[4]{0:T(128)} %anc_ref.1, bf16[96,640]{1,0:T(8,128)(2,1)} %bitcast.3, f32[640]{0:T(1024)} %scale_hbm.1, f32[640]{0:T(1024)} %shift_hbm.1, bf16[720,640]{1,0:T(8,128)(2,1)} %wconv_hbm.1, bf16[640,1920]{1,0:T(8,128)(2,1)} %wqkv_hbm.1, bf16[640,640]{1,0:T(8,128)(2,1)} %wout_hbm.1), custom_call_target="tpu_custom_call" | custom-call | tf_op jit(solution)/shard_map/block/pallas_call | solution.py:591
  50.2 1.6 %copy.9 = bf16[1,4,24,640]{3,2,1,0:T(8,128)(2,1)} copy(bf16[1,4,24,640]{3,2,1,0:T(8,128)(2,1)} %bitcast.2) | data formatting | bytes 245760

commit v3 on v2

--- a/solution.py
+++ b/solution.py
@@ -13,6 +13,11 @@
 INNER = 2
 CUT1 = 2
 CUT2 = 1
+HOP1 = 0
+HOP2 = 0
+STRAIGHT = 2
+WIDE = 2
+DIRECT2 = 0
 CORES = 2
 LANES = 128
 GRAIN = 16
@@ -46,7 +51,10 @@
     wd,
     wqkv,
     wpad,
-    wkvt,
+    wnear,
+    wmid,
+    wlate,
+    kacc,
     wout,
     lat,
     act,
@@ -60,20 +68,28 @@
     blocks,
     stat_own,
     stats,
+    norm_own,
+    norms,
     load_sem,
+    ns,
+    nr,
     ws,
     wr,
     ss,
     sent1,
     near1,
     far1,
+    turned1,
+    side1,
     sent2,
     near2,
     far2,
+    turned2,
+    side2,
     ps,
     pr,
 ):
-    rows_here, width, chans, ranks, particles, share = dims
+    rows_here, width, chans, ranks, particles, share, early = dims
     tokens = rows_here * width
     total = tokens * ranks
     outer = ranks // INNER
@@ -168,76 +184,124 @@
         )
 
     class Gather:
-        def __init__(self, src, buf, rows, cuts, sent, near, far):
+        def __init__(self, src, buf, rows, cuts, hop, sent, near, far, turned, side_far):
             self.src, self.buf, self.rows, self.cuts = src, buf, rows, cuts
             self.sent, self.near, self.far = sent, near, far
+            self.turned, self.side_far = turned, side_far
+            self.hop = hop
+            self.hop_rows = cuts[hop][0]
             self.pieces = range(len(cuts))
 
         def rows_of(self, slot, start, size):
             return self.buf.at[pl.ds(pl.multiple_of(slot * self.rows + start, GRAIN), size)]
 
-        def onto(self, origin, i, side, own=False):
+        def send(self, slot, i, side, recv, own=False):
             start, size = self.cuts[i]
-            dst = self.rows_of(origin * INNER + b, start, size)
+            dst = self.rows_of(slot, start, size)
             src = self.src.at[pl.ds(start, size)] if own else dst
-            recv = self.near.at[origin, i] if side else self.far.at[origin]
             row = (a + side) * INNER + b if side else other
             return remote(src, dst, self.sent.at[side + 1], recv, {"rows": row})
 
-        def pass_on(self, origin, i, side, own=False):
-            onward = (a + 1 < outer) if side == 1 else (a > 0)
-
-            @pl.when(onward)
-            def _():
-                self.onto(origin, i, side, own).start()
+        def along(self, origin, i, side, own=False):
+            return self.send(origin * INNER + b, i, side, self.near.at[origin, i], own)
+
+        def across(self, origin, i, own=False):
+            recv = self.turned.at[i] if own and i < self.hop else self.far.at[origin]
+            return self.send(origin * INNER + b, i, 0, recv, own)
 
         def begin(self, pieces):
             for i in pieces:
-                self.onto(a, i, 0, True).start()
-                self.pass_on(a, i, 1, True)
-                self.pass_on(a, i, -1, True)
+                self.across(a, i, True).start()
+                for side, onward in ((1, a + 1 < outer), (-1, a > 0)):
+
+                    @pl.when(onward)
+                    def _():
+                        self.along(a, i, side, True).start()
 
         def keep(self):
             self.buf[pl.ds(pl.multiple_of(me * self.rows, GRAIN), self.rows)] = self.src[...]
 
-        def step(self, t):
-            for i in self.pieces:
-                for present, origin, side in ((a >= t, a - t, 1), (a + t < outer, a + t, -1)):
+        def turn(self):
+            for i in range(self.hop):
+                self.send(other, i, 0, self.turned.at[i]).wait_recv()
+                for side, onward in ((1, a + 1 < outer), (-1, a > 0)):
+
+                    @pl.when(onward)
+                    def _():
+                        self.send(other, i, side, self.side_far.at[(1 + side) // 2]).start()
+
+        def sides(self, t):
+            return ((a >= t, a - t, 1, a + 1 < outer), (a + t < outer, a + t, -1, a > 0))
+
+        def order(self, t):
+            return list(self.pieces)
+
+        def step(self, t, pieces=None):
+            for i in self.pieces if pieces is None else pieces:
+                for present, origin, side, onward in self.sides(t):
 
                     @pl.when(present)
                     def _():
-                        self.onto(origin, i, 1).wait_recv()
-                        self.pass_on(origin, i, side)
-                        self.onto(origin, i, 0).start()
-
-        def far_slab(self, origin):
-            slab = self.rows_of(origin * INNER + (1 - b), 0, self.rows)
-            remote(slab, slab, self.sent.at[1], self.far.at[origin], {"rows": other}).wait_recv()
+                        self.along(origin, i, 1).wait_recv()
+
+                        @pl.when(onward)
+                        def _():
+                            self.along(origin, i, side).start()
+
+                        if t > 1 or i >= self.hop:
+                            self.across(origin, i).start()
+
+        def got(self, slot, start, size, recv):
+            part = self.rows_of(slot, start, size)
+            remote(part, part, self.sent.at[1], recv, {"rows": other}).wait_recv()
 
         def rest(self, t):
             if t == 0:
-                self.far_slab(a)
+                self.got(other, self.hop_rows, self.rows - self.hop_rows, self.far.at[a])
                 return
-            for present, origin in ((a >= t, a - t), (a + t < outer, a + t)):
+            for present, origin, side, _ in self.sides(t):
+                slot = origin * INNER + (1 - b)
 
                 @pl.when(present)
                 def _():
-                    self.far_slab(origin)
-
-        def sent_all(self, side, slabs):
-            part = self.buf.at[0 : slabs * self.rows]
+                    if t > 1 or not self.hop:
+                        self.got(slot, 0, self.rows, self.far.at[origin])
+                    else:
+                        top = self.hop_rows
+                        self.got(slot, 0, top, self.side_far.at[(1 + side) // 2])
+                        self.got(slot, top, self.rows - top, self.far.at[origin])
+
+        def sent_all(self, side, rows):
+            part = self.buf.at[0:rows]
             remote(part, part, self.sent.at[side + 1], self.far.at[0], {"rows": other}).wait_send()
 
         def finish(self):
-            self.sent_all(0, outer)
             for v in range(outer):
 
                 @pl.when(a == v)
                 def _():
+                    beside = (v > 0) + (v + 1 < outer)
+                    self.sent_all(0, outer * self.rows - beside * self.hop_rows)
                     if v + 1 < outer:
-                        self.sent_all(1, v + 1)
+                        self.sent_all(1, (v + 1) * self.rows + self.hop_rows)
                     if v > 0:
-                        self.sent_all(-1, outer - v)
+                        self.sent_all(-1, (outer - v) * self.rows + self.hop_rows)
+
+    def each_of(t, column, fn):
+        if t == 0:
+            fn(a * INNER + column)
+            return
+        for present, origin in ((a >= t, a - t), (a + t < outer, a + t)):
+
+            @pl.when(present)
+            def _():
+                fn(origin * INNER + column)
+
+    def each_near(t, fn):
+        each_of(t, b, fn)
+
+    def each_far(t, fn):
+        each_of(t, 1 - b, fn)
 
     def each_slot(t, fn):
         if t == 0:
@@ -252,8 +316,9 @@
                 fn(origin * INNER + (1 - b))
 
     near_half = outer // 2
-    first = Gather(x_ref, lat, tokens, cut_rows(tokens, CUT1), sent1, near1, far1)
-    second = Gather(chunk, rt, csp, cut_rows(csp, CUT2), sent2, near2, far2)
+    hop2 = min(HOP2, csp // (CUT2 * GRAIN) - 1)
+    first = Gather(x_ref, lat, tokens, cut_rows(tokens, CUT1), HOP1, sent1, near1, far1, turned1, side1)
+    second = Gather(chunk, rt, csp, cut_rows(csp, CUT2), hop2, sent2, near2, far2, turned2, side2)
 
     def stat_copy(k):
         return remote(
@@ -287,13 +352,19 @@
     with jax.named_scope("start"):
         for k in range(1, ranks):
             stat_copy(k).start()
-        for k in range(1, ranks):
+        for k in range(particles, ranks):
 
             @pl.when(mine == k % particles)
             def _():
                 w_copy(k).start()
 
         first.begin(first.pieces)
+        for k in range(1, particles):
+
+            @pl.when(mine == k % particles)
+            def _():
+                w_copy(k).start()
+
         first.keep()
         wbuf[me] = wt[me]
 
@@ -322,9 +393,26 @@
         def _():
             w_arrived(k)
 
-    with jax.named_scope("w1"):
-        for k in range(1, ranks):
-            w_forward(k)
+    low_end = a < near_half
+    with jax.named_scope("kvw"):
+        loads[1].wait()
+        if cpad != chans:
+            wqkv[...] = jnp.zeros_like(wqkv)
+            for d in range(ranks):
+                wqkv[d * csp : d * csp + cs] = wpad[d * cs : (d + 1) * cs]
+        late = INNER * csp
+        near_size = cpad // 2
+        parts = (
+            (jnp.where(low_end, 0, near_size), near_size, wnear),
+            (jnp.where(low_end, near_size, late), near_size - late, wmid),
+            (jnp.where(low_end, cpad - late, 0), late, wlate),
+        )
+        parts = [(pl.multiple_of(at, GRAIN), size, dst) for at, size, dst in parts]
+        for at, size, dst in parts:
+            for n in range(2 * tiles):
+                dst[n * LANES : (n + 1) * LANES] = wqkv[
+                    pl.ds(at, size), chans + n * LANES : chans + (n + 1) * LANES
+                ].T
     with jax.named_scope("g1a"):
         for t in range(1, near_half):
             first.step(t)
@@ -356,14 +444,20 @@
             wd[...], act[pl.ds(at, half)], NT, preferred_element_type=f32
         )
 
+    with jax.named_scope("wf2"):
+        for k in range(particles, ranks):
+            w_forward(k)
     with jax.named_scope("own"):
         activate(me)
-    with jax.named_scope("g1b"):
+    with jax.named_scope("g1b0"):
         for t in range(near_half, outer - 1):
-            first.step(t)
-    with jax.named_scope("w2"):
-        for k in range(1, ranks):
-            w_relay(k)
+            first.step(t, first.order(t)[:1])
+    with jax.named_scope("wf1"):
+        for k in range(1, min(particles, ranks)):
+            w_forward(k)
+    with jax.named_scope("g1b1"):
+        for t in range(near_half, outer - 1):
+            first.step(t, first.order(t)[1:])
     with jax.named_scope("act1"):
         first.rest(0)
         activate(other)
@@ -372,6 +466,9 @@
             each_slot(t, activate)
     with jax.named_scope("g1c"):
         first.step(outer - 1)
+    with jax.named_scope("w2"):
+        for k in range(1, ranks):
+            w_relay(k)
     with jax.named_scope("act2"):
         for t in range(near_half, outer - 1):
             first.rest(t)
@@ -431,9 +528,13 @@
     same = jnp.where(same, 1.0, 0.0).astype(f32)
     lane = lax.broadcasted_iota(jnp.int32, (csp, LANES), 1)
 
-    def normalize(slot):
-        at = pl.ds(pl.multiple_of(slot * csp, GRAIN), csp)
-        v = rt[at].astype(f32)
+    def norm_copy(k):
+        return remote(
+            norm_own, norms.at[me], ns.at[0], nr.at[me], {"rows": lax.rem(me + k, ranks)}
+        )
+
+    with jax.named_scope("own"):
+        v = chunk[...].astype(f32)
         both = jnp.where(
             lane == 0,
             jnp.sum(v, axis=1, keepdims=True),
@@ -442,43 +543,66 @@
         both = jnp.dot(same, both, precision=HIGH, preferred_element_type=f32) / count
         mean = both[:, 0:1]
         inv = lax.rsqrt(both[:, 1:2] - mean * mean + 1e-05)
-        nt[at] = ((v - mean) * inv).astype(bf16)
+        both = jnp.where(lane == 0, mean, jnp.where(lane == 1, inv, 0.0))
+        both = jnp.concatenate([both, jnp.zeros((LANES - csp, LANES), f32)], axis=0)
+        norm_own[...] = both.T[0:8]
+        for k in range(1, ranks):
+            norm_copy(k).start()
+        nt[pl.ds(pl.multiple_of(me * csp, GRAIN), csp)] = ((v - mean) * inv).astype(bf16)
+
+    def normalize(slot):
+        at = pl.ds(pl.multiple_of(slot * csp, GRAIN), csp)
+        remote(norm_own, norms.at[slot], ns.at[0], nr.at[slot], {"rows": other}).wait_recv()
+        both = norms[slot].T
+        v = rt[at].astype(f32)
+        nt[at] = ((v - both[:csp, 0:1]) * both[:csp, 1:2]).astype(bf16)
+
+    step = 2 * LANES
+    kv_rows = [slice(n * step, (n + 1) * step) for n in range(2 * chans // step)]
+
+    def kv_part(i, rows):
+        at, size, weights = parts[i]
+        return jnp.dot(weights[rows], nt[pl.ds(at, size)], preferred_element_type=f32)
 
     with jax.named_scope("g2"):
-        loads[1].wait()
-        if cpad != chans:
-            wqkv[...] = jnp.zeros_like(wqkv)
-            for d in range(ranks):
-                wqkv[d * csp : d * csp + cs] = wpad[d * cs : (d + 1) * cs]
-        for n in range(2 * tiles):
-            wkvt[n * LANES : (n + 1) * LANES] = wqkv[
-                :, chans + n * LANES : chans + (n + 1) * LANES
-            ].T
-        normalize(me)
         for t in range(1, outer):
             second.step(t)
-        second.rest(0)
-        normalize(other)
-        for t in range(1, outer):
-            second.rest(t)
-            each_slot(t, normalize)
-
-    with jax.named_scope("qkv"):
-        step = 2 * LANES
-        for n in range(2 * chans // step):
-            kvt[n * step : (n + 1) * step] = jnp.dot(
-                wkvt[n * step : (n + 1) * step], nt[...], preferred_element_type=f32
-            ).astype(bf16)
+            second.rest(t - 1)
+            each_far(t - 1, normalize)
+            each_near(t, normalize)
+            if early and t == near_half:
+                for rows in kv_rows:
+                    kacc[rows] = kv_part(0, rows)
+
+    with jax.named_scope("kv1"):
         row = lax.broadcasted_iota(jnp.int32, (tokens, total), 0)
         at = lax.broadcasted_iota(jnp.int32, (tokens, total), 1)
         pick = jnp.where(at == me * tokens + row, 1.0, 0.0).astype(bf16)
-        mine_n = lax.dot_general(pick, nt[...], NT, preferred_element_type=f32).astype(bf16)
+
+        def query_part(i):
+            at, size, _ = parts[i]
+            at = pl.ds(at, size)
+            own = lax.dot_general(pick, nt[at], NT, preferred_element_type=f32).astype(bf16)
+            return jnp.dot(own, wqkv[at, :chans], preferred_element_type=f32)
+
+        query = query_part(0) + query_part(1)
+        if early:
+            for rows in kv_rows:
+                kacc[rows] += kv_part(1, rows)
+    with jax.named_scope("g2b"):
+        second.rest(outer - 1)
+        each_far(outer - 1, normalize)
+
+    with jax.named_scope("qkv"):
+        query = (query + query_part(2)).astype(bf16)
+        for rows in kv_rows:
+            head = kacc[rows] if early else kv_part(0, rows) + kv_part(1, rows)
+            kvt[rows] = (head + kv_part(2, rows)).astype(bf16)
         resid = lax.dot_general(pick, rt[...], NT, preferred_element_type=f32)
         if cpad != chans:
             resid = jnp.concatenate(
                 [resid[:, d * csp : d * csp + cs] for d in range(ranks)], axis=1
             )
-        query = jnp.dot(mine_n, wqkv[:, :chans], preferred_element_type=f32).astype(bf16)
 
     with jax.named_scope("attn"):
         pair = 2 * head_dim
@@ -508,19 +632,25 @@
             ).astype(bf16)
     def to_core(p, j):
         where = {"particle": grp * CORES + (1 - core)}
-        return remote(blocks.at[p, j], blocks.at[p, j], ps.at[0], pr.at[0, 0], where)
-
-    def to_group(j, g):
-        where = {"particle": lax.rem(grp + g, groups) * CORES + core}
-        return remote(blocks.at[mine, j], blocks.at[mine, j], ps.at[g], pr.at[g, j], where)
+        return remote(blocks.at[p * tiles + j], blocks.at[p * tiles + j], ps.at[0], pr.at[0, 0], where)
+
+    def to_group(j, g, cross=0):
+        there = 1 - core if cross else core
+        where = {"particle": lax.rem(grp + g, groups) * CORES + there}
+        recv = pr.at[0, 1] if cross else pr.at[g, j]
+        return remote(blocks.at[mine * tiles + j], blocks.at[mine * tiles + j], ps.at[groups if cross else g], recv, where)
 
     def from_group(j, g):
-        part = blocks.at[of_group(g, core), j]
+        part = blocks.at[of_group(g, core) * tiles + j]
         remote(part, part, ps.at[g], pr.at[g, j], {"rows": other}).wait_recv()
 
-    def whole_blocks(n, sem):
+    def tiles_of(n, sem, recv=0):
         part = blocks.at[0:n]
-        return remote(part, part, ps.at[sem], pr.at[0, 0], {"rows": other})
+        return remote(part, part, ps.at[sem], pr.at[0, recv], {"rows": other})
+
+    passed = max(0, tiles - STRAIGHT)
+    by_core = tiles + (groups - 1) * passed
+    crossing = (groups - 1) * (tiles - passed)
 
     def of_group(g, side):
         return lax.rem(grp + groups - g, groups) * CORES + side
@@ -528,29 +658,42 @@
     with jax.named_scope("proj"):
         loads[2].wait()
         for j in range(tiles):
-            at = slice(j * LANES, (j + 1) * LANES)
-            blocks[mine, j] = (
-                resid[:, at] + jnp.dot(att[...], wout[:, at], preferred_element_type=f32)
-            ).astype(bf16)
+            if j % WIDE == 0:
+                at = slice(j * LANES, min(j + WIDE, tiles) * LANES)
+                wide = resid[:, at] + jnp.dot(
+                    att[...], wout[:, at], preferred_element_type=f32
+                )
+            at = j % WIDE * LANES
+            blocks[mine * tiles + j] = wide[:, at : at + LANES].astype(bf16)
             for g in range(1, groups):
                 to_group(j, g).start()
             to_core(mine, j).start()
+        for j in range(passed, tiles):
+            for g in range(1, groups):
+                to_group(j, g, 1).start()
 
     with jax.named_scope("resample"):
         for j in range(tiles):
             for g in range(1, groups):
                 from_group(j, g)
-                to_core(of_group(g, core), j).start()
-        whole_blocks(groups, 0).wait_recv()
+                if j < passed:
+                    to_core(of_group(g, core), j).start()
+        tiles_of(by_core, 0).wait_recv()
+        if crossing:
+            tiles_of(crossing, 0, 1).wait_recv()
         for j in range(tiles):
-            out_ref[:, j * LANES : (j + 1) * LANES] = blocks[anc_ref[mine], j]
+            out_ref[:, j * LANES : (j + 1) * LANES] = blocks[anc_ref[mine] * tiles + j]
     with jax.named_scope("drain"):
-        whole_blocks(groups, 0).wait_send()
+        tiles_of(by_core, 0).wait_send()
         for g in range(1, groups):
-            whole_blocks(1, g).wait_send()
+            tiles_of(tiles, g).wait_send()
+        if crossing:
+            tiles_of(crossing, groups).wait_send()
         first.finish()
         second.finish()
         stat_all().wait_send()
+        part = norms.at[0 : ranks - 1]
+        remote(part, part, ns.at[0], nr.at[0], {"rows": other}).wait_send()
         for q in range(particles):
             count = len(range(q, ranks, particles)) - (q == 0)
 
@@ -585,7 +728,8 @@
     cpad = csp * ranks
     outer = ranks // INNER
     n1, n2 = len(cut_rows(tokens, CUT1)), len(cut_rows(csp, CUT2))
-    dims = (rows_here, width, chans, ranks, particles, share)
+    early = outer <= 4
+    dims = (rows_here, width, chans, ranks, particles, share, early)
     bf16, f32 = jnp.bfloat16, jnp.float32
     dma = pltpu.SemaphoreType.DMA
     out = pl.pallas_call(
@@ -604,7 +748,10 @@
             pltpu.VMEM((TAPS * csp, chans), bf16),
             pltpu.VMEM((cpad, 3 * chans), bf16),
             pltpu.VMEM((GRAIN, LANES) if cpad == chans else qkv_weight.shape, bf16),
-            pltpu.VMEM((2 * chans, cpad), bf16),
+            pltpu.VMEM((2 * chans, cpad // 2), bf16),
+            pltpu.VMEM((2 * chans, cpad // 2 - INNER * csp), bf16),
+            pltpu.VMEM((2 * chans, INNER * csp), bf16),
+            pltpu.VMEM((2 * chans, total) if early else (8, LANES), f32),
             pltpu.VMEM(out_weight.shape, bf16),
             pltpu.VMEM((total, chans), bf16),
             pltpu.VMEM((total, chans), bf16),
@@ -615,20 +762,28 @@
             pltpu.VMEM((cpad, total), bf16),
             pltpu.VMEM((2 * chans, total), bf16),
             pltpu.VMEM((tokens, chans), bf16),
-            pltpu.VMEM((particles, chans // LANES, tokens, LANES), bf16),
+            pltpu.VMEM((particles * (chans // LANES), tokens, LANES), bf16),
+            pltpu.VMEM((8, LANES), f32),
+            pltpu.VMEM((ranks, 8, LANES), f32),
             pltpu.VMEM((8, LANES), f32),
             pltpu.VMEM((ranks, 8, LANES), f32),
             dma((6,)),
+            dma((1,)),
+            dma((ranks,)),
             dma((1 + groups,)),
             dma((ranks,)),
             dma((2,)),
             dma((3,)),
             dma((outer, n1)),
             dma((outer,)),
+            dma((max(1, HOP1),)),
+            dma((2,)),
             dma((3,)),
             dma((outer, n2)),
             dma((outer,)),
-            dma((groups,)),
+            dma((max(1, HOP2),)),
+            dma((2,)),
+            dma((groups + 1,)),
             dma((groups, chans // LANES)),
         ],
         compiler_params=pltpu.CompilerParams(

time: 52 us -> 50.1 us (0.963)
  Pallas kernels: 50.2 us -> 48.4 us
    pallas_call x1, Pallas kernels: 50.2 us -> 48.4 us  [per_device(): pl.pallas_call(functools.partial(kernel, dims), out_shape=jax.ShapeDtypeS...]
where the time goes in v3:
time: 50.1 us; the launch traced here: 50 us
  Pallas kernels  48.4 us (97%)
  local copies, waits for them, and re-layouts  1.56 us (3%)
    pallas_call x1, Pallas kernels, per_device(): pl.pallas_call(functools.partial(kernel, dims), out_shape=jax.ShapeDtypeS...  48.4 us
    unnamed x1, local copies, waits for them, and re-layouts  1.56 us

profile of v3, /device:TPU:0, one launch (start us, length us, event | category | flops | bytes accessed | tf_op | source)
XLA Modules:
  0.0 50.0 jit_solution(12085042023506910740)
XLA Ops:
  0.0 48.4 %block.1 = bf16[96,640]{1,0:T(8,128)(2,1)} custom-call(s32[4]{0:T(128)} %anc_ref.1, bf16[96,640]{1,0:T(8,128)(2,1)} %bitcast.3, f32[640]{0:T(1024)} %scale_hbm.1, f32[640]{0:T(1024)} %shift_hbm.1, bf16[720,640]{1,0:T(8,128)(2,1)} %wconv_hbm.1, bf16[640,1920]{1,0:T(8,128)(2,1)} %wqkv_hbm.1, bf16[640,640]{1,0:T(8,128)(2,1)} %wout_hbm.1), custom_call_target="tpu_custom_call" | custom-call | tf_op jit(solution)/shard_map/block/pallas_call | solution.py:735
  48.4 1.6 %copy.9 = bf16[1,4,24,640]{3,2,1,0:T(8,128)(2,1)} copy(bf16[1,4,24,640]{3,2,1,0:T(8,128)(2,1)} %bitcast.2) | data formatting | bytes 245760

commit v4 on v3

--- a/solution.py
+++ b/solution.py
@@ -13,8 +13,6 @@
 INNER = 2
 CUT1 = 2
 CUT2 = 1
-HOP1 = 0
-HOP2 = 0
 STRAIGHT = 2
 WIDE = 2
 DIRECT2 = 0
@@ -79,13 +77,9 @@
     sent1,
     near1,
     far1,
-    turned1,
-    side1,
     sent2,
     near2,
     far2,
-    turned2,
-    side2,
     ps,
     pr,
 ):
@@ -162,14 +156,6 @@
     stat_own[...] = jnp.dot(sums, to_group, precision=HIGH, preferred_element_type=f32)
     stats[me] = stat_own[...]
 
-    with jax.named_scope("turn"):
-        loads[0].wait()
-        turned = wz[...].T
-        for d in range(ranks):
-            wt[d, 0:cs] = turned[d * cs : (d + 1) * cs]
-            if csp != cs:
-                wt[d, cs:csp] = jnp.zeros((csp - cs, wt.shape[2]), bf16)
-
     with jax.named_scope("barrier"):
         pl.semaphore_wait(barrier, ranks + particles - 2)
 
@@ -184,12 +170,9 @@
         )
 
     class Gather:
-        def __init__(self, src, buf, rows, cuts, hop, sent, near, far, turned, side_far):
+        def __init__(self, src, buf, rows, cuts, sent, near, far):
             self.src, self.buf, self.rows, self.cuts = src, buf, rows, cuts
             self.sent, self.near, self.far = sent, near, far
-            self.turned, self.side_far = turned, side_far
-            self.hop = hop
-            self.hop_rows = cuts[hop][0]
             self.pieces = range(len(cuts))
 
         def rows_of(self, slot, start, size):
@@ -206,8 +189,7 @@
             return self.send(origin * INNER + b, i, side, self.near.at[origin, i], own)
 
         def across(self, origin, i, own=False):
-            recv = self.turned.at[i] if own and i < self.hop else self.far.at[origin]
-            return self.send(origin * INNER + b, i, 0, recv, own)
+            return self.send(origin * INNER + b, i, 0, self.far.at[origin], own)
 
         def begin(self, pieces):
             for i in pieces:
@@ -221,15 +203,6 @@
         def keep(self):
             self.buf[pl.ds(pl.multiple_of(me * self.rows, GRAIN), self.rows)] = self.src[...]
 
-        def turn(self):
-            for i in range(self.hop):
-                self.send(other, i, 0, self.turned.at[i]).wait_recv()
-                for side, onward in ((1, a + 1 < outer), (-1, a > 0)):
-
-                    @pl.when(onward)
-                    def _():
-                        self.send(other, i, side, self.side_far.at[(1 + side) // 2]).start()
-
         def sides(self, t):
             return ((a >= t, a - t, 1, a + 1 < outer), (a + t < outer, a + t, -1, a > 0))
 
@@ -248,28 +221,21 @@
                         def _():
                             self.along(origin, i, side).start()
 
-                        if t > 1 or i >= self.hop:
-                            self.across(origin, i).start()
-
-        def got(self, slot, start, size, recv):
-            part = self.rows_of(slot, start, size)
-            remote(part, part, self.sent.at[1], recv, {"rows": other}).wait_recv()
+                        self.across(origin, i).start()
+
+        def far_slab(self, origin):
+            slab = self.rows_of(origin * INNER + (1 - b), 0, self.rows)
+            remote(slab, slab, self.sent.at[1], self.far.at[origin], {"rows": other}).wait_recv()
 
         def rest(self, t):
             if t == 0:
-                self.got(other, self.hop_rows, self.rows - self.hop_rows, self.far.at[a])
+                self.far_slab(a)
                 return
-            for present, origin, side, _ in self.sides(t):
-                slot = origin * INNER + (1 - b)
+            for present, origin, _, _ in self.sides(t):
 
                 @pl.when(present)
                 def _():
-                    if t > 1 or not self.hop:
-                        self.got(slot, 0, self.rows, self.far.at[origin])
-                    else:
-                        top = self.hop_rows
-                        self.got(slot, 0, top, self.side_far.at[(1 + side) // 2])
-                        self.got(slot, top, self.rows - top, self.far.at[origin])
+                    self.far_slab(origin)
 
         def sent_all(self, side, rows):
             part = self.buf.at[0:rows]
@@ -280,12 +246,11 @@
 
                 @pl.when(a == v)
                 def _():
-                    beside = (v > 0) + (v + 1 < outer)
-                    self.sent_all(0, outer * self.rows - beside * self.hop_rows)
+                    self.sent_all(0, outer * self.rows)
                     if v + 1 < outer:
-                        self.sent_all(1, (v + 1) * self.rows + self.hop_rows)
+                        self.sent_all(1, (v + 1) * self.rows)
                     if v > 0:
-                        self.sent_all(-1, (outer - v) * self.rows + self.hop_rows)
+                        self.sent_all(-1, (outer - v) * self.rows)
 
     def each_of(t, column, fn):
         if t == 0:
@@ -316,9 +281,8 @@
                 fn(origin * INNER + (1 - b))
 
     near_half = outer // 2
-    hop2 = min(HOP2, csp // (CUT2 * GRAIN) - 1)
-    first = Gather(x_ref, lat, tokens, cut_rows(tokens, CUT1), HOP1, sent1, near1, far1, turned1, side1)
-    second = Gather(chunk, rt, csp, cut_rows(csp, CUT2), hop2, sent2, near2, far2, turned2, side2)
+    first = Gather(x_ref, lat, tokens, cut_rows(tokens, CUT1), sent1, near1, far1)
+    second = Gather(chunk, rt, csp, cut_rows(csp, CUT2), sent2, near2, far2)
 
     def stat_copy(k):
         return remote(
@@ -352,13 +316,23 @@
     with jax.named_scope("start"):
         for k in range(1, ranks):
             stat_copy(k).start()
+        first.begin(first.pieces)
+
+    with jax.named_scope("turn"):
+        loads[0].wait()
+        turned = wz[...].T
+        for d in range(ranks):
+            wt[d, 0:cs] = turned[d * cs : (d + 1) * cs]
+            if csp != cs:
+                wt[d, cs:csp] = jnp.zeros((csp - cs, wt.shape[2]), bf16)
+
+    with jax.named_scope("start2"):
         for k in range(particles, ranks):
 
             @pl.when(mine == k % particles)
             def _():
                 w_copy(k).start()
 
-        first.begin(first.pieces)
         for k in range(1, particles):
 
             @pl.when(mine == k % particles)
@@ -632,21 +606,21 @@
             ).astype(bf16)
     def to_core(p, j):
         where = {"particle": grp * CORES + (1 - core)}
-        return remote(blocks.at[p * tiles + j], blocks.at[p * tiles + j], ps.at[0], pr.at[0, 0], where)
+        return remote(blocks.at[p * tiles + j], blocks.at[p * tiles + j], ps.at[0], pr.at[0], where)
 
     def to_group(j, g, cross=0):
         there = 1 - core if cross else core
         where = {"particle": lax.rem(grp + g, groups) * CORES + there}
-        recv = pr.at[0, 1] if cross else pr.at[g, j]
+        recv = pr.at[1] if cross else pr.at[2 + (g - 1) * tiles + j]
         return remote(blocks.at[mine * tiles + j], blocks.at[mine * tiles + j], ps.at[groups if cross else g], recv, where)
 
     def from_group(j, g):
         part = blocks.at[of_group(g, core) * tiles + j]
-        remote(part, part, ps.at[g], pr.at[g, j], {"rows": other}).wait_recv()
+        remote(part, part, ps.at[g], pr.at[2 + (g - 1) * tiles + j], {"rows": other}).wait_recv()
 
     def tiles_of(n, sem, recv=0):
         part = blocks.at[0:n]
-        return remote(part, part, ps.at[sem], pr.at[0, recv], {"rows": other})
+        return remote(part, part, ps.at[sem], pr.at[recv], {"rows": other})
 
     passed = max(0, tiles - STRAIGHT)
     by_core = tiles + (groups - 1) * passed
@@ -734,7 +708,7 @@
     dma = pltpu.SemaphoreType.DMA
     out = pl.pallas_call(
         functools.partial(kernel, dims),
-        out_shape=jax.ShapeDtypeStruct((tokens, chans), bf16),
+        out_shape=pltpu.VMEM((tokens, chans), bf16),
         in_specs=[pl.BlockSpec(memory_space=pltpu.SMEM)]
         + [pl.BlockSpec(memory_space=pl.ANY)] * 6,
         out_specs=pl.BlockSpec(memory_space=pltpu.VMEM),
@@ -776,15 +750,11 @@
             dma((3,)),
             dma((outer, n1)),
             dma((outer,)),
-            dma((max(1, HOP1),)),
-            dma((2,)),
             dma((3,)),
             dma((outer, n2)),
             dma((outer,)),
-            dma((max(1, HOP2),)),
-            dma((2,)),
             dma((groups + 1,)),
-            dma((groups, chans // LANES)),
+            dma((2 + (groups - 1) * (chans // LANES),)),
         ],
         compiler_params=pltpu.CompilerParams(
             collective_id=0, has_side_effects=True, vmem_limit_bytes=64000 * 1024

time: 50.1 us -> 48.5 us (0.968)
  local copies, waits for them, and re-layouts: 1.56 us -> 0.65 us
  Pallas kernels: 48.4 us -> 47.7 us
    unnamed x1, local copies, waits for them, and re-layouts: 1.56 us -> 0.65 us
    pallas_call x1, Pallas kernels: 48.4 us -> 47.7 us  [per_device(): pl.pallas_call(functools.partial(kernel, dims), out_shape=pltpu.VMEM((tok...]
where the time goes in v4:
time: 48.5 us; the launch traced here: 48.4 us
  Pallas kernels  47.7 us (98%)
  local copies, waits for them, and re-layouts  0.65 us (1%)
    pallas_call x1, Pallas kernels, per_device(): pl.pallas_call(functools.partial(kernel, dims), out_shape=pltpu.VMEM((tok...  47.7 us

profile of v4, /device:TPU:0, one launch (start us, length us, event | category | flops | bytes accessed | tf_op | source)
XLA Modules:
  0.0 48.4 jit_solution(13719727566482653854)
XLA Ops:
  0.0 47.7 %block.1 = bf16[96,640]{1,0:T(8,128)(2,1)S(1)} custom-call(s32[4]{0:T(128)} %anc_ref.1, bf16[96,640]{1,0:T(8,128)(2,1)} %bitcast.3, f32[640]{0:T(1024)} %scale_hbm.1, f32[640]{0:T(1024)} %shift_hbm.1, bf16[720,640]{1,0:T(8,128)(2,1)} %wconv_hbm.1, bf16[640,1920]{1,0:T(8,128)(2,1)} %wqkv_hbm.1, bf16[640,640]{1,0:T(8,128)(2,1)} %wout_hbm.1), custom_call_target="tpu_custom_call" | custom-call | tf_op jit(solution)/shard_map/block/pallas_call | solution.py:709
  47.7 0.7 %copy.9 = bf16[1,4,24,640]{3,2,1,0:T(8,128)(2,1)} copy(bf16[1,4,24,640]{3,2,1,0:T(8,128)(2,1)S(1)} %bitcast.2) | data formatting | bytes 245760

commit v5 on v4

--- a/solution.py
+++ b/solution.py
@@ -63,6 +63,7 @@
     nt,
     kvt,
     att,
+    own_rows,
     blocks,
     stat_own,
     stats,
@@ -95,6 +96,7 @@
     count = total * per_group
     head_dim = chans // HEADS
     tiles = chans // LANES
+    fold = math.log2(head_dim) % 2 == 0
     bf16, f32 = jnp.bfloat16, jnp.float32
     me = lax.axis_index("rows")
     mine = lax.axis_index("particle")
@@ -327,13 +329,13 @@
                 wt[d, cs:csp] = jnp.zeros((csp - cs, wt.shape[2]), bf16)
 
     with jax.named_scope("start2"):
+        for k in range(1, particles):
+
+            @pl.when(mine == k % particles)
+            def _():
+                w_copy(k).start()
+
         for k in range(particles, ranks):
-
-            @pl.when(mine == k % particles)
-            def _():
-                w_copy(k).start()
-
-        for k in range(1, particles):
 
             @pl.when(mine == k % particles)
             def _():
@@ -418,16 +420,16 @@
             wd[...], act[pl.ds(at, half)], NT, preferred_element_type=f32
         )
 
-    with jax.named_scope("wf2"):
-        for k in range(particles, ranks):
-            w_forward(k)
     with jax.named_scope("own"):
         activate(me)
+    with jax.named_scope("wf1"):
+        for k in range(1, min(particles, ranks)):
+            w_forward(k)
     with jax.named_scope("g1b0"):
         for t in range(near_half, outer - 1):
             first.step(t, first.order(t)[:1])
-    with jax.named_scope("wf1"):
-        for k in range(1, min(particles, ranks)):
+    with jax.named_scope("wf2"):
+        for k in range(particles, ranks):
             w_forward(k)
     with jax.named_scope("g1b1"):
         for t in range(near_half, outer - 1):
@@ -560,6 +562,18 @@
             return jnp.dot(own, wqkv[at, :chans], preferred_element_type=f32)
 
         query = query_part(0) + query_part(1)
+        if cpad == chans:
+            ahead = pl.ds(pl.multiple_of(jnp.where(low_end, 0, late), GRAIN), cpad - late)
+            own = lax.dot_general(pick, rt[ahead], NT, preferred_element_type=f32)
+
+            @pl.when(low_end)
+            def _():
+                own_rows[:, : chans - late] = own
+
+            @pl.when(jnp.logical_not(low_end))
+            def _():
+                own_rows[:, late:] = own
+
         if early:
             for rows in kv_rows:
                 kacc[rows] += kv_part(1, rows)
@@ -569,12 +583,27 @@
 
     with jax.named_scope("qkv"):
         query = (query + query_part(2)).astype(bf16)
+        if fold:
+            query = (query.astype(f32) * head_dim ** (-0.5)).astype(bf16)
         for rows in kv_rows:
             head = kacc[rows] if early else kv_part(0, rows) + kv_part(1, rows)
             kvt[rows] = (head + kv_part(2, rows)).astype(bf16)
-        resid = lax.dot_general(pick, rt[...], NT, preferred_element_type=f32)
-        if cpad != chans:
-            resid = jnp.concatenate(
+        if cpad == chans:
+            own = lax.dot_general(
+                pick, rt[pl.ds(parts[2][0], late)], NT, preferred_element_type=f32
+            )
+
+            @pl.when(low_end)
+            def _():
+                own_rows[:, chans - late :] = own
+
+            @pl.when(jnp.logical_not(low_end))
+            def _():
+                own_rows[:, :late] = own
+
+        else:
+            resid = lax.dot_general(pick, rt[...], NT, preferred_element_type=f32)
+            own_rows[...] = jnp.concatenate(
                 [resid[:, d * csp : d * csp + cs] for d in range(ranks)], axis=1
             )
 
@@ -588,7 +617,9 @@
             q = jnp.concatenate([jnp.where(low, q, zero), jnp.where(low, zero, q)], axis=0)
             scores = jnp.dot(
                 q, kvt[h * pair : (h + 1) * pair], preferred_element_type=f32
-            ) * (head_dim ** (-0.5))
+            )
+            if not fold:
+                scores = scores * (head_dim ** (-0.5))
             top = jnp.max(scores, axis=1, keepdims=True)
             weights = jnp.exp(scores - top)
             norm = jnp.sum(weights, axis=1, keepdims=True)
@@ -634,7 +665,7 @@
         for j in range(tiles):
             if j % WIDE == 0:
                 at = slice(j * LANES, min(j + WIDE, tiles) * LANES)
-                wide = resid[:, at] + jnp.dot(
+                wide = own_rows[:, at] + jnp.dot(
                     att[...], wout[:, at], preferred_element_type=f32
                 )
             at = j % WIDE * LANES
@@ -736,6 +767,7 @@
             pltpu.VMEM((cpad, total), bf16),
             pltpu.VMEM((2 * chans, total), bf16),
             pltpu.VMEM((tokens, chans), bf16),
+            pltpu.VMEM((tokens, chans), f32),
             pltpu.VMEM((particles * (chans // LANES), tokens, LANES), bf16),
             pltpu.VMEM((8, LANES), f32),
             pltpu.VMEM((ranks, 8, LANES), f32),

time: 48.5 us -> 48.2 us (level)
  no operation moved by 1% of the time
where the time goes in v5:
time: 48.2 us; the launch traced here: 48.1 us
  Pallas kernels  47.4 us (98%)
  local copies, waits for them, and re-layouts  0.65 us (1%)
    pallas_call x1, Pallas kernels, per_device(): pl.pallas_call(functools.partial(kernel, dims), out_shape=pltpu.VMEM((tok...  47.4 us

profile of v5, /device:TPU:0, one launch (start us, length us, event | category | flops | bytes accessed | tf_op | source)
XLA Modules:
  0.0 48.1 jit_solution(4035660474539968213)
XLA Ops:
  0.0 47.4 %block.1 = bf16[96,640]{1,0:T(8,128)(2,1)S(1)} custom-call(s32[4]{0:T(128)} %anc_ref.1, bf16[96,640]{1,0:T(8,128)(2,1)} %bitcast.3, f32[640]{0:T(1024)} %scale_hbm.1, f32[640]{0:T(1024)} %shift_hbm.1, bf16[720,640]{1,0:T(8,128)(2,1)} %wconv_hbm.1, bf16[640,1920]{1,0:T(8,128)(2,1)} %wqkv_hbm.1, bf16[640,640]{1,0:T(8,128)(2,1)} %wout_hbm.1), custom_call_target="tpu_custom_call" | custom-call | tf_op jit(solution)/shard_map/block/pallas_call | solution.py:740
  47.4 0.7 %copy.9 = bf16[1,4,24,640]{3,2,1,0:T(8,128)(2,1)} copy(bf16[1,4,24,640]{3,2,1,0:T(8,128)(2,1)S(1)} %bitcast.2) | data formatting | bytes 245760

commit v6 on v5

--- a/solution.py
+++ b/solution.py
@@ -145,19 +145,6 @@
     inside = (chan_c >= group_c) & (chan_c < group_c + per_group)
     to_chan = jnp.where(inside, 1.0, 0.0).astype(f32)
 
-    loads[3].wait()
-    x32 = x_ref[...].astype(f32)
-    sums = jnp.concatenate(
-        [
-            jnp.sum(x32, axis=0, keepdims=True),
-            jnp.sum(x32 * x32, axis=0, keepdims=True),
-            jnp.zeros((6, chans), f32),
-        ],
-        axis=0,
-    )
-    stat_own[...] = jnp.dot(sums, to_group, precision=HIGH, preferred_element_type=f32)
-    stats[me] = stat_own[...]
-
     with jax.named_scope("barrier"):
         pl.semaphore_wait(barrier, ranks + particles - 2)
 
@@ -316,9 +303,22 @@
         return w_pass_on(k, 1 + g, {"particle": lax.rem(grp + g, groups) * CORES + core})
 
     with jax.named_scope("start"):
+        loads[3].wait()
+        first.begin(first.pieces[:1])
+        x32 = x_ref[...].astype(f32)
+        sums = jnp.concatenate(
+            [
+                jnp.sum(x32, axis=0, keepdims=True),
+                jnp.sum(x32 * x32, axis=0, keepdims=True),
+                jnp.zeros((6, chans), f32),
+            ],
+            axis=0,
+        )
+        stat_own[...] = jnp.dot(sums, to_group, precision=HIGH, preferred_element_type=f32)
+        stats[me] = stat_own[...]
         for k in range(1, ranks):
             stat_copy(k).start()
-        first.begin(first.pieces)
+        first.begin(first.pieces[1:])
 
     with jax.named_scope("turn"):
         loads[0].wait()

time: 48.2 us -> 48.3 us (level)
  no operation moved by 1% of the time
where the time goes in v6:
time: 48.3 us; the launch traced here: 48.1 us
  Pallas kernels  47.4 us (98%)
  local copies, waits for them, and re-layouts  0.65 us (1%)
    pallas_call x1, Pallas kernels, per_device(): pl.pallas_call(functools.partial(kernel, dims), out_shape=pltpu.VMEM((tok...  47.4 us

profile of v6, /device:TPU:0, one launch (start us, length us, event | category | flops | bytes accessed | tf_op | source)
XLA Modules:
  0.0 48.1 jit_solution(11089160512568167638)
XLA Ops:
  0.0 47.4 %block.1 = bf16[96,640]{1,0:T(8,128)(2,1)S(1)} custom-call(s32[4]{0:T(128)} %anc_ref.1, bf16[96,640]{1,0:T(8,128)(2,1)} %bitcast.3, f32[640]{0:T(1024)} %scale_hbm.1, f32[640]{0:T(1024)} %shift_hbm.1, bf16[720,640]{1,0:T(8,128)(2,1)} %wconv_hbm.1, bf16[640,1920]{1,0:T(8,128)(2,1)} %wqkv_hbm.1, bf16[640,640]{1,0:T(8,128)(2,1)} %wout_hbm.1), custom_call_target="tpu_custom_call" | custom-call | tf_op jit(solution)/shard_map/block/pallas_call | solution.py:740
  47.5 0.7 %copy.9 = bf16[1,4,24,640]{3,2,1,0:T(8,128)(2,1)} copy(bf16[1,4,24,640]{3,2,1,0:T(8,128)(2,1)S(1)} %bitcast.2) | data formatting | bytes 245760
